TPU v7x, 256 devices: a whole 4x4x8 slice. The times are simulated.
256 devices in a mesh: row: 8 (over z_hi, y), col: 32 (over x, z_lo, core).
Axes of the slice: x: 4, y: 4, z: 8 (z_hi: 2, z_lo: 4; z = z_hi * 4 + z_lo), core: 2. Of those that a mesh axis runs over, the one named last changes fastest.
Arguments:
- features: bfloat16 [65536, 256], P('col', 'row'), may hold values from -6 to 6
- block_values: bfloat16 [8, 32, 256, 128, 128], P('row', 'col'), may hold values from -0.046875 to 0.046875
- block_coords: int32 [8, 32, 2, 256], P('row', 'col'), may hold values from 0 to 63, as said below
- live_blocks: int32 [8, 32], P('row', 'col'), may hold values from 32 to 256, as said below
- weight: bfloat16 [256, 256], replicated, may hold values from -0.375 to 0.375
- bias: float32 [256], replicated, may hold values from -3 to 3
- cotangent: bfloat16 [65536, 256], P(('row', 'col')), may hold values from -6 to 6
Outputs:
- out: bfloat16 [65536, 256], P(('row', 'col'))
- grad_x: bfloat16 [65536, 256], P('col', 'row')
- grad_weight: float32 [256, 256], replicated
- grad_bias: float32 [256], replicated
Inputs may be any that keep to these rules, and one draw needn't show every extreme that they name: `block_coords`: within one tile the 256 slots name distinct pairs of a row block (0 to 63) and a column block (0 to 15). Only the first live_blocks[i, j] slots of tile (i, j) belong to the adjacency; some tile has all 256 slots live.
All inputs are finite; a program needn't handle non-finite values.
Results may differ from a plain program's by a relative error of at most 0.0075.
Values may be sent and summed in bfloat16 or wider, within the bound.
A program may use at most 128 MiB of HBM per device.

v0:
```python
import math

import jax
import jax.numpy as jnp
from jax import lax
from jax.sharding import PartitionSpec as P


def block_products(block_vals, source, dst_index, src_index, live_count, out_blocks, transposed):
    slot_total = block_vals.shape[0]
    block_size = block_vals.shape[1]
    feat_width = source.shape[2]
    group_size = math.gcd(slot_total, 64)
    pattern = "sab,saf->sbf" if transposed else "sab,sbf->saf"
    offsets = jnp.arange(group_size, dtype=jnp.int32)

    def one_group(turn, totals):
        first_slot = turn * group_size
        slab_vals = lax.dynamic_slice_in_dim(block_vals, first_slot, group_size, 0)
        take_from = lax.dynamic_slice_in_dim(src_index, first_slot, group_size, 0)
        put_to = lax.dynamic_slice_in_dim(dst_index, first_slot, group_size, 0)
        picked = jnp.take(source, take_from, axis=0)
        products = jnp.einsum(pattern, slab_vals, picked, preferred_element_type=jnp.float32)
        alive_mask = first_slot + offsets < live_count
        products = jnp.where(alive_mask[:, None, None], products, 0.0)
        return totals.at[put_to].add(products)

    start_totals = jnp.zeros((out_blocks, block_size, feat_width), jnp.float32)
    turns = slot_total // group_size
    return lax.fori_loop(0, turns, one_group, start_totals)


def on_device(features, block_values, block_coords, live_blocks, weight, bias, cotangent):
    block_vals = block_values[0, 0]
    row_ids = block_coords[0, 0, 0]
    col_ids = block_coords[0, 0, 1]
    live_count = live_blocks[0, 0]
    block_size = block_vals.shape[1]
    feat_width = weight.shape[0]
    col_count = lax.axis_size("col")
    feat_tile = lax.all_gather(features, "row", axis=1, tiled=True)
    col_blocks = feat_tile.shape[0] // block_size
    row_blocks = cotangent.shape[0] * col_count // block_size
    feat_blocks = feat_tile.reshape(col_blocks, block_size, feat_width)
    partial_value = block_products(
        block_vals, feat_blocks, row_ids, col_ids, live_count, row_blocks, False
    )
    partial_value = partial_value.reshape(row_blocks * block_size, feat_width)
    aggregate = lax.psum_scatter(partial_value, "col", scatter_dimension=0, tiled=True).astype(
        jnp.bfloat16
    )
    preact = jnp.dot(aggregate, weight, preferred_element_type=jnp.float32) + bias
    sigmoid_v = jax.nn.sigmoid(preact)
    out = (preact * sigmoid_v).astype(jnp.bfloat16)
    derivative = sigmoid_v * (1.0 + preact * (1.0 - sigmoid_v))
    grad_pre = (cotangent.astype(jnp.float32) * derivative).astype(jnp.bfloat16)
    weight_term = lax.dot_general(
        aggregate, grad_pre, (((0,), (0,)), ((), ())), preferred_element_type=jnp.float32
    )
    bias_term = jnp.sum(grad_pre.astype(jnp.float32), axis=0)
    weight_sum, bias_sum = lax.psum((weight_term, bias_term), ("row", "col"))
    norm_factor = (feat_tile.shape[0] * col_count) ** (-0.5)
    grad_weight = weight_sum * norm_factor
    grad_bias = bias_sum * norm_factor
    grad_agg = lax.dot_general(
        grad_pre, weight, (((1,), (1,)), ((), ())), preferred_element_type=jnp.float32
    ).astype(jnp.bfloat16)
    grad_tile = lax.all_gather(grad_agg, "col", axis=0, tiled=True)
    grad_blocks = grad_tile.reshape(row_blocks, block_size, feat_width)
    partial_x = block_products(
        block_vals, grad_blocks, col_ids, row_ids, live_count, col_blocks, True
    )
    partial_x = partial_x.reshape(col_blocks * block_size, feat_width)
    grad_x = lax.psum_scatter(partial_x, "row", scatter_dimension=1, tiled=True).astype(
        jnp.bfloat16
    )
    return (out, grad_x, grad_weight, grad_bias)


def solution(mesh):
    in_specs = (
        P("col", "row"),
        P("row", "col", None, None, None),
        P("row", "col", None, None),
        P("row", "col"),
        P(),
        P(),
        P(("row", "col"), None),
    )
    out_specs = (P(("row", "col"), None), P("col", "row"), P(), P())
    return jax.shard_map(
        on_device, mesh=mesh, in_specs=in_specs, out_specs=out_specs, check_vma=False
    )
```

profile of v0, /device:TPU:1, one launch (start us, length us, event | category | flops | bytes accessed | tf_op | source)
XLA Modules:
  0.0 784.1 jit_solution(2173765968436024874)
XLA Ops:
  7.2 0.7 all-gather.3.cloned.1.call-update
  8.0 0.8 fusion.27
  8.7 66.2 %all-gather.3.cloned.1.call-done = bf16[2048,256]{0,1:T(8,128)(2,1)} async-done(((bf16[2048,32]{0,1:T(8,128)(2,1)}), bf16[2048,256]{0,1:T(8,128)(2,1)}) %all-gather.3.cloned.1.call-update) | async-done | bytes 1048592 | tf_op jit(solution)/shard_map/all_gather | solution.py:41
  75.0 1.5 copy.12
  76.5 4.2 broadcast_in_dim.123
  80.7 122.1 %while.28 = (s32[]{:T(128)}, f32[64,128,256]{2,1,0:T(8,128)}, s32[256]{0:T(256)S(1)}, s32[]{:T(128)}, bf16[256,128,128]{2,1,0:T(8,128)(2,1)}, /*index=5*/s32[256...) while((s32[]{:T(128)}, f32[64,128,256]{2,1,0:T(8,128)}, ...), condition=%wide.region_2.3_spmd.clone, body=%wide.region_0.2_spmd.clone.sunk | while | flops 543164096 | bytes 48240816 | solution.py:30
  80.7 0.7 compare_and_fusion.4
  81.4 2.8 gather_fusion
  84.2 7.4 broadcast_select_fusion.4
  91.6 0.1 compare_select_fusion.8
  91.6 19.8 %scatter_fusion = f32[64,128,256]{2,1,0:T(8,128)} fusion(f32[64,128,256]{2,1,0:T(8,128)} %get-tuple-element.472, s32[64]{0:T(128)S(1)} %compare_select_fusion.8, f32[64,128,256]{2,1,0:T(8,128)} %broadcast_select_fusion.4), kind=kCustom, calls=%fused_computation.2.clone.clone.1 | custom fusion | flops 2097152 | bytes 25166080 | tf_op jit(solution)/shard_map/while/body/eval_jaxpr/scatter-add | solution.py:26
  111.4 0.7 compare_and_fusion.4
  112.2 2.8 gather_fusion
  114.9 7.4 broadcast_select_fusion.4
  122.3 0.1 compare_select_fusion.8
  122.3 19.5 %scatter_fusion = f32[64,128,256]{2,1,0:T(8,128)} fusion(f32[64,128,256]{2,1,0:T(8,128)} %get-tuple-element.472, s32[64]{0:T(128)S(1)} %compare_select_fusion.8, f32[64,128,256]{2,1,0:T(8,128)} %broadcast_select_fusion.4), kind=kCustom, calls=%fused_computation.2.clone.clone.1 | custom fusion | flops 2097152 | bytes 25166080 | tf_op jit(solution)/shard_map/while/body/eval_jaxpr/scatter-add | solution.py:26
  141.9 0.7 compare_and_fusion.4
  142.6 2.8 gather_fusion
  145.4 7.4 broadcast_select_fusion.4
  152.7 0.1 compare_select_fusion.8
  152.8 19.5 %scatter_fusion = f32[64,128,256]{2,1,0:T(8,128)} fusion(f32[64,128,256]{2,1,0:T(8,128)} %get-tuple-element.472, s32[64]{0:T(128)S(1)} %compare_select_fusion.8, f32[64,128,256]{2,1,0:T(8,128)} %broadcast_select_fusion.4), kind=kCustom, calls=%fused_computation.2.clone.clone.1 | custom fusion | flops 2097152 | bytes 25166080 | tf_op jit(solution)/shard_map/while/body/eval_jaxpr/scatter-add | solution.py:26
  172.3 0.7 compare_and_fusion.4
  173.0 2.8 gather_fusion
  175.8 7.4 broadcast_select_fusion.4
  183.1 0.1 compare_select_fusion.8
  183.2 19.6 %scatter_fusion = f32[64,128,256]{2,1,0:T(8,128)} fusion(f32[64,128,256]{2,1,0:T(8,128)} %get-tuple-element.472, s32[64]{0:T(128)S(1)} %compare_select_fusion.8, f32[64,128,256]{2,1,0:T(8,128)} %broadcast_select_fusion.4), kind=kCustom, calls=%fused_computation.2.clone.clone.1 | custom fusion | flops 2097152 | bytes 25166080 | tf_op jit(solution)/shard_map/while/body/eval_jaxpr/scatter-add | solution.py:26
  202.9 0.0 all-gather.5.cloned.1.call-start
  202.9 155.9 %reduce-scatter.3.cloned.1.call-done = f32[256,256]{1,0:T(8,128)} async-done(((f32[8192,256]{1,0:T(8,128)}), f32[256,256]{1,0:T(8,128)}) %reduce-scatter.3.cloned.1.call-update) | async-done | bytes 262160 | tf_op jit(solution)/shard_map/reduce_scatter | solution.py:49
  358.8 1.9 convert_reduce_fusion
  360.7 0.9 convolution_convert_fusion
  361.7 0.0 all-reduce.2.cloned.1.call-start
  361.7 12.0 %copy.11 = bf16[1,1,256,128,128]{3,4,2,1,0:T(8,128)(2,1)} copy(bf16[1,1,256,128,128]{4,3,2,1,0:T(8,128)(2,1)} %bitcast.18) | data formatting | bytes 16777216 | tf_op args[1]
  373.7 0.9 fusion.24
  374.7 0.0 reduce-scatter.5.cloned.1.call-start
  374.7 50.0 %all-gather.5.cloned.1.call-done = bf16[8192,256]{1,0:T(8,128)(2,1)} async-done(((bf16[256,256]{1,0:T(8,128)(2,1)}), bf16[8192,256]{1,0:T(8,128)(2,1)}) %all-gather.5.cloned.1.call-update) | async-done | bytes 4194320 | tf_op jit(solution)/shard_map/all_gather | solution.py:68
  424.7 0.2 broadcast_in_dim.124
  424.9 102.6 %while.29 = (s32[]{:T(128)}, f32[16,128,256]{2,1,0:T(8,128)S(1)}, s32[256]{0:T(256)S(1)}, s32[]{:T(128)}, bf16[256,128,128]{1,2,0:T(8,128)(2,1)}, /*index=5*/s32...) while((s32[]{:T(128)}, f32[16,128,256]{2,1,0:T(8,128)S(1)}, ...), condition=%wide.region_6.7_spmd.clone, body=%wide.region_4.6_spmd.clone.sunk | while | flops 543164096 | bytes 48240816 | solution.py:30
  424.9 0.7 compare_and_fusion.5
  425.7 5.0 gather_fusion.1
  430.6 7.4 broadcast_select_fusion.5
  438.0 0.1 compare_select_fusion.9
  438.1 12.5 %scatter_fusion.1 = f32[16,128,256]{2,1,0:T(8,128)S(1)} fusion(f32[16,128,256]{2,1,0:T(8,128)S(1)} %get-tuple-element.505, s32[64]{0:T(128)S(1)} %compare_select_fusion.9, f32[64,128,256]{2,1,0:T(8,128)} %broadcast_select_fusion.5), kind=kCustom, calls=%fused_computation.3.clone.clone.1 | custom fusion | flops 2097152 | bytes 25166080 | tf_op jit(solution)/shard_map/while/body/eval_jaxpr/scatter-add | solution.py:26
  450.5 0.7 compare_and_fusion.5
  451.3 5.0 gather_fusion.1
  456.3 7.4 broadcast_select_fusion.5
  463.6 0.1 compare_select_fusion.9
  463.7 12.5 %scatter_fusion.1 = f32[16,128,256]{2,1,0:T(8,128)S(1)} fusion(f32[16,128,256]{2,1,0:T(8,128)S(1)} %get-tuple-element.505, s32[64]{0:T(128)S(1)} %compare_select_fusion.9, f32[64,128,256]{2,1,0:T(8,128)} %broadcast_select_fusion.5), kind=kCustom, calls=%fused_computation.3.clone.clone.1 | custom fusion | flops 2097152 | bytes 25166080 | tf_op jit(solution)/shard_map/while/body/eval_jaxpr/scatter-add | solution.py:26
  476.2 0.7 compare_and_fusion.5
  477.0 5.0 gather_fusion.1
  481.9 7.4 broadcast_select_fusion.5
  489.3 0.1 compare_select_fusion.9
  489.4 12.4 %scatter_fusion.1 = f32[16,128,256]{2,1,0:T(8,128)S(1)} fusion(f32[16,128,256]{2,1,0:T(8,128)S(1)} %get-tuple-element.505, s32[64]{0:T(128)S(1)} %compare_select_fusion.9, f32[64,128,256]{2,1,0:T(8,128)} %broadcast_select_fusion.5), kind=kCustom, calls=%fused_computation.3.clone.clone.1 | custom fusion | flops 2097152 | bytes 25166080 | tf_op jit(solution)/shard_map/while/body/eval_jaxpr/scatter-add | solution.py:26
  501.9 0.7 compare_and_fusion.5
  502.6 5.0 gather_fusion.1
  507.6 7.4 broadcast_select_fusion.5
  514.9 0.1 compare_select_fusion.9
  515.0 12.4 %scatter_fusion.1 = f32[16,128,256]{2,1,0:T(8,128)S(1)} fusion(f32[16,128,256]{2,1,0:T(8,128)S(1)} %get-tuple-element.505, s32[64]{0:T(128)S(1)} %compare_select_fusion.9, f32[64,128,256]{2,1,0:T(8,128)} %broadcast_select_fusion.5), kind=kCustom, calls=%fused_computation.3.clone.clone.1 | custom fusion | flops 2097152 | bytes 25166080 | tf_op jit(solution)/shard_map/while/body/eval_jaxpr/scatter-add | solution.py:26
  527.5 1.9 copy.16
  529.3 76.7 %psum.15 = f32[256]{0:T(256)S(1)} all-reduce(f32[256]{0:T(256)S(1)} %get-tuple-element.355), channel_id=1, replica_groups=mesh['row'=8,'col'=32] {'row','col'}, use_global_device_ids=true, to_apply=%region_10.11 | all-reduce | flops 256 | bytes 2048 | tf_op jit(solution)/shard_map/psum | solution.py:61
  606.0 0.6 broadcast_multiply_fusion.1
  606.6 71.5 %all-reduce.2.cloned.1.call-done = f32[256,256]{1,0:T(8,128)} async-done(((f32[256,256]{1,0:T(8,128)}), f32[256,256]{1,0:T(8,128)}) %all-reduce.2.cloned.1.call-update) | async-done | bytes 262160 | tf_op jit(solution)/shard_map/psum | solution.py:61
  678.1 1.7 broadcast_multiply_fusion
  679.8 96.2 %reduce-scatter.5.cloned.1.call-done = f32[2048,32]{0,1:T(8,128)} async-done(((f32[2048,256]{0,1:T(8,128)}), f32[2048,32]{0,1:T(8,128)}) %reduce-scatter.5.cloned.1.call-update) | async-done | bytes 262160 | tf_op jit(solution)/shard_map/reduce_scatter | solution.py:74
  776.0 1.6 convert_element_type.26
  (22 shorter events, 0.2 us)
Async XLA Ops:
  7.2 351.7 %copy-start = (bf16[256,256]{1,0:T(8,128)(2,1)S(1)}, bf16[256,256]{1,0:T(8,128)(2,1)}, u32[]{:S(2)}) copy-start(bf16[256,256]{1,0:T(8,128)(2,1)} %param.15) | copy-start | bytes 393220
  7.2 67.8 %all-gather.3.cloned.1.call-start = ((), (), s32[]{:S(2)}) async-start(), calls=%async_computation.2 | async-start | bytes 1179648 | tf_op jit(solution)/shard_map/all_gather | solution.py:41
  7.9 350.9 %reduce-scatter.3.cloned.1.call-start = ((), (), s32[]{:S(2)}) async-start(), calls=%async_computation.3 | async-start | bytes 8650752 | tf_op jit(solution)/shard_map/reduce_scatter | solution.py:49
  202.8 156.0 %copy-start.2 = (bf16[256,256]{1,0:T(8,128)(2,1)S(1)}, bf16[256,256]{1,0:T(8,128)(2,1)}, u32[]{:S(2)}) copy-start(bf16[256,256]{1,0:T(8,128)(2,1)} %param.17) | copy-start | bytes 393220
  202.8 156.0 %copy-start.3 = (f32[256]{0:T(256)S(1)}, f32[256]{0:T(256)}, u32[]{:S(2)}) copy-start(f32[256]{0:T(256)} %param.16) | copy-start | bytes 3076
  202.9 221.8 %all-gather.5.cloned.1.call-start = ((), (), s32[]{:S(2)}) async-start(), calls=%async_computation.4 | async-start | bytes 4325376 | tf_op jit(solution)/shard_map/all_gather | solution.py:68
  361.6 12.1 %copy-start.1 = (f32[256,256]{1,0:T(8,128)S(1)}, f32[256,256]{1,0:T(8,128)}, u32[]{:S(2)}) copy-start(f32[256,256]{1,0:T(8,128)} %reduce-scatter.3.cloned.1.call-done) | copy-start | bytes 786436
  361.7 316.4 %all-reduce.2.cloned.1.call-start = ((), (), s32[]{:S(2)}) async-start(), calls=%async_computation.6 | async-start | bytes 524288 | tf_op jit(solution)/shard_map/psum | solution.py:61
  374.7 401.3 %reduce-scatter.5.cloned.1.call-start = ((), (), s32[]{:S(2)}) async-start(), calls=%async_computation.5 | async-start | bytes 2359296 | tf_op jit(solution)/shard_map/reduce_scatter | solution.py:74
Sparse Core Ops, SparseCore 0:
  10.6 64.2 all-gather.2
  203.0 155.7 reduce-scatter.2
  361.8 62.8 all-gather.4
  430.6 247.4 all-reduce.1
  682.0 93.9 reduce-scatter.4
where the time goes:
time: 786 us; the launch traced here: 784 us
  waiting for transfers between devices  441 us (56%)
  other arithmetic  139 us (18%)
  blocking collectives  76.7 us (10%)
  matrix products  62.7 us (8%)
  local copies, waits for them, and re-layouts  51.4 us (7%)
  between operations  13.8 us (2%)
    reduce_scatter x1, waiting for transfers between devices, on_device(): lax.psum_scatter(partial_value, 'col', scatter_dimension=0, tiled=True)  156 us
    scatter-add x8, other arithmetic, one_group(): return totals.at[put_to].add(products)  128 us
    reduce_scatter x1, waiting for transfers between devices, on_device(): lax.psum_scatter(partial_x, 'row', scatter_dimension=1, tiled=True)  96.2 us
    psum x1, blocking collectives, on_device(): weight_sum, bias_sum = lax.psum((weight_term, bias_term), ('row', 'col'))  76.7 us
    psum x1, waiting for transfers between devices, on_device(): weight_sum, bias_sum = lax.psum((weight_term, bias_term), ('row', 'col'))  71.5 us
    all_gather x1, waiting for transfers between devices, on_device(): feat_tile = lax.all_gather(features, 'row', axis=1, tiled=True)  66.2 us
    dot_general x8, matrix products, one_group(): jnp.einsum(pattern, slab_vals, picked, preferred_element_type=jnp.float32)  59 us
    all_gather x1, waiting for transfers between devices, on_device(): grad_tile = lax.all_gather(grad_agg, 'col', axis=0, tiled=True)  50 us
  transfers between devices with their start and end apart: 5, of which 5 were waited for; matrix products, arithmetic and copies ran while one was open for 15% of the time, Pallas kernels for 0%

commit v1 on v0

v1 whole, which is shorter than its diff:
```python
import functools

import jax
import jax.numpy as jnp
from jax import lax
from jax.experimental import pallas as pl
from jax.experimental.pallas import tpu as pltpu
from jax.sharding import PartitionSpec as P

MESH = pl.DeviceIdType.MESH
F32 = jnp.float32
BF16 = jnp.bfloat16
VMEM_LIMIT = 64000000
GROUP = 32
UNROLL = 4


def place():
    row, col = lax.axis_index("row"), lax.axis_index("col")
    return row // 4, row % 4, col // 8, (col // 2) % 4, col % 2


def device(zh, y, x, zl, core):
    return (zh * 4 + y, (x * 4 + zl) * 2 + core)


def copy_to(src, dst, sends, recvs, at, dev):
    return pltpu.make_async_remote_copy(
        src_ref=src,
        dst_ref=dst,
        send_sem=sends.at[at],
        recv_sem=recvs.at[at],
        device_id=dev,
        device_id_type=MESH,
    )


def meet(devices):
    barrier = pltpu.get_barrier_semaphore()
    for dev in devices:
        pl.semaphore_signal(barrier, inc=1, device_id=dev, device_id_type=MESH)
    pl.semaphore_wait(barrier, len(devices))


def rem4(v):
    return lax.rem(v, 4)


def gather_rows_kernel(x_ref, full_ref, sends, recvs):
    zh, y, x, zl, core = place()
    right = device(zh, rem4(y + 1), x, zl, core)
    left = device(zh, rem4(y + 3), x, zl, core)
    across = device(1 - zh, y, x, zl, core)
    meet((left, right, across))
    mine = zh * 4 + y
    other = (1 - zh) * 4 + y
    halves = (pl.ds(0, 16), pl.ds(16, 16))
    started = []

    def start(c):
        c.start()
        started.append(c)
        return c

    zc = [
        start(copy_to(x_ref.at[h], full_ref.at[mine, h], sends, recvs, 12 + i, across))
        for i, h in enumerate(halves)
    ]
    full_ref[mine] = x_ref[...]
    firsts = []
    for k in range(2):
        me = mine if k == 0 else other
        base = (zh if k == 0 else 1 - zh) * 4
        src = x_ref if k == 0 else full_ref.at[other]

        def ring(h, at, dev):
            return start(
                copy_to(src.at[halves[h]], full_ref.at[me, halves[h]], sends, recvs, k * 6 + at, dev)
            )

        if k == 1:
            zc[0].wait_recv()
        r0 = ring(0, 0, right)
        if k == 1:
            zc[1].wait_recv()
        l1 = ring(1, 1, left)
        r1 = ring(1, 2, right)
        l0 = ring(0, 3, left)
        firsts.append((r0, l1, r1, l0, base))
        if k == 0:
            continue
    forwards = []
    for k in range(2):
        r0, l1, r1, l0, base = firsts[k]
        from_left = base + rem4(y + 3)
        from_right = base + rem4(y + 1)
        r0.wait_recv()
        fr = start(
            copy_to(
                full_ref.at[from_left, halves[0]],
                full_ref.at[from_left, halves[0]],
                sends,
                recvs,
                k * 6 + 4,
                right,
            )
        )
        l1.wait_recv()
        fl = start(
            copy_to(
                full_ref.at[from_right, halves[1]],
                full_ref.at[from_right, halves[1]],
                sends,
                recvs,
                k * 6 + 5,
                left,
            )
        )
        forwards += [r1, l0, fr, fl]
    for c in forwards:
        c.wait_recv()
    for c in started:
        c.wait_send()


def gather_rows(x_t):
    width, verts = x_t.shape
    return pl.pallas_call(
        gather_rows_kernel,
        out_shape=jax.ShapeDtypeStruct((8, width, verts), BF16),
        in_specs=[pl.BlockSpec(memory_space=pltpu.VMEM)],
        out_specs=pl.BlockSpec(memory_space=pltpu.VMEM),
        scratch_shapes=[pltpu.SemaphoreType.DMA((14,)), pltpu.SemaphoreType.DMA((14,))],
        compiler_params=pltpu.CompilerParams(
            collective_id=0, has_side_effects=True, vmem_limit_bytes=VMEM_LIMIT
        ),
        name="gather_features",
    )(x_t)


def forward_kernel(rows, cols, live, a_ref, xt_ref, out_ref, xs, acc):
    g = pl.program_id(0)
    n_rb = acc.shape[0] - 1
    n_cb = xs.shape[0]

    @pl.when(g == 0)
    def _():
        for c in range(n_cb):
            xs[c] = xt_ref[:, c * 128 : (c + 1) * 128].T

        def clear(i, _):
            acc[i] = jnp.zeros(acc.shape[1:], F32)
            return 0

        lax.fori_loop(0, n_rb, clear, 0)

    count = jnp.clip(live[0] - g * GROUP, 0, GROUP)

    def some(q, _):
        products = []
        for u in range(UNROLL):
            s = q * UNROLL + u
            products.append(
                jnp.dot(a_ref[s], xs[cols[g * GROUP + s]], preferred_element_type=F32)
            )
        for u in range(UNROLL):
            s = g * GROUP + q * UNROLL + u
            r = jnp.where(s < live[0], rows[s], n_rb)
            acc[r] += products[u]
        return 0

    lax.fori_loop(0, (count + UNROLL - 1) // UNROLL, some, 0)

    @pl.when(g == pl.num_programs(0) - 1)
    def _():
        def put(chip, _):
            for k in range(4):
                out_ref[k // 2, chip, (k % 2) * 128 : (k % 2 + 1) * 128, :] = acc[chip * 4 + k].astype(BF16)
            return 0

        lax.fori_loop(0, 16, put, 0)


def forward_products(rows, cols, live, blocks, x_t):
    n_slots = blocks.shape[0]
    return pl.pallas_call(
        forward_kernel,
        out_shape=jax.ShapeDtypeStruct((2, 16, 256, 256), BF16),
        grid_spec=pltpu.PrefetchScalarGridSpec(
            num_scalar_prefetch=3,
            grid=(n_slots // GROUP,),
            in_specs=[
                pl.BlockSpec((GROUP, 128, 128), lambda g, *_: (g, 0, 0)),
                pl.BlockSpec((256, 2048), lambda g, *_: (0, 0)),
            ],
            out_specs=pl.BlockSpec((2, 16, 256, 256), lambda g, *_: (0, 0, 0, 0)),
            scratch_shapes=[pltpu.VMEM((16, 128, 256), BF16), pltpu.VMEM((65, 128, 256), F32)],
        ),
        compiler_params=pltpu.CompilerParams(vmem_limit_bytes=VMEM_LIMIT),
        name="forward_products",
    )(rows, cols, live, blocks, x_t)


def middle_kernel(
    part, cot_ref, w_ref, bias_ref, out_ref, full_ref, term_ref,
    r_a, s_a, r_b1l, r_b1r, r_b2l, r_b2r, s_b, r_c, sends, recvs,
):
    zh, y, x, zl, core = place()
    right = device(zh, y, rem4(x + 1), zl, core)
    left = device(zh, y, rem4(x + 3), zl, core)
    twin = device(zh, y, x, zl, 1 - core)
    along = [None] + [device(zh, y, x, rem4(zl + k), core) for k in range(1, 4)]
    meet((left, right, twin, along[1], along[2], along[3]))
    started = []
    used = [0]

    def start(src, dst, dev):
        c = copy_to(src, dst, sends, recvs, used[0], dev)
        used[0] += 1
        c.start()
        started.append(c)
        return c

    top, low = pl.ds(0, 128), pl.ds(128, 128)
    xk = [rem4(x + k) for k in range(4)]
    zk = [rem4(zl + k) for k in range(4)]
    order = (1, 2, 3, 0)
    a = {}
    for k in (2, 1, 3, 0):
        sl = pl.ds(xk[k] * 4, 4)
        a[k] = start(part.at[1 - core, sl], r_a.at[sl], twin)

    def add_cores(k):
        a[k].wait_recv()

        def one(z, _):
            i = xk[k] * 4 + z
            s_a[i] = (part[core, i].astype(F32) + r_a[i].astype(F32)).astype(BF16)
            return 0

        lax.fori_loop(0, 4, one, 0)

    add_cores(2)
    b1 = {}
    for k in order:
        i = xk[2] * 4 + zk[k]
        b1[k] = (
            start(s_a.at[i, top], r_b1l.at[k], right),
            start(s_a.at[i, low], r_b1r.at[k], left),
        )
    b2 = {}
    add_cores(1)
    for k in order:
        b2[k] = [start(s_a.at[xk[1] * 4 + zk[k], low], r_b2l.at[k, low], right)]
    add_cores(3)
    for k in order:
        b2[k].append(start(s_a.at[xk[3] * 4 + zk[k], top], r_b2r.at[k, top], left))
    for k in order:
        b1[k][0].wait_recv()
        i = xk[1] * 4 + zk[k]
        s_a[i, top] = (s_a[i, top].astype(F32) + r_b1l[k].astype(F32)).astype(BF16)
        b2[k].append(start(s_a.at[i, top], r_b2l.at[k, top], right))
        b1[k][1].wait_recv()
        j = xk[3] * 4 + zk[k]
        s_a[j, low] = (s_a[j, low].astype(F32) + r_b1r[k].astype(F32)).astype(BF16)
        b2[k].append(start(s_a.at[j, low], r_b2r.at[k, low], left))
    add_cores(0)
    c_z = {}
    total = None
    for k in order:
        for c in b2[k]:
            c.wait_recv()
        i = x * 4 + zk[k]
        value = s_a[i].astype(F32) + (r_b2l[k].astype(F32) + r_b2r[k].astype(F32))
        if k == 0:
            total = value
        else:
            s_b[k] = value.astype(BF16)
            c_z[k] = start(s_b.at[k], r_c.at[k], along[k])
    for k in (1, 2, 3):
        c_z[k].wait_recv()
        total = total + r_c[k].astype(F32)
    aggregate = total.astype(BF16)
    preact = jnp.dot(aggregate, w_ref[...], preferred_element_type=F32) + bias_ref[...]
    sig = jax.nn.sigmoid(preact)
    derivative = sig * (1.0 + preact * (1.0 - sig))
    grad_pre = (cot_ref[...].astype(F32) * derivative).astype(BF16)
    grad_agg = lax.dot_general(
        w_ref[...], grad_pre, (((1,), (1,)), ((), ())), preferred_element_type=F32
    ).astype(BF16)
    mine = (x * 4 + zl) * 2 + core
    full_ref[mine, 0] = grad_agg[:, 0:128]
    full_ref[mine, 1] = grad_agg[:, 128:256]

    def at(xx, zz):
        return (xx * 4 + zz) * 2 + core

    def ring(d):
        here = full_ref
        return (
            start(here.at[d, 0], here.at[d, 0], right),
            start(here.at[d, 1], here.at[d, 1], left),
            start(here.at[d, 1], here.at[d, 1], right),
            start(here.at[d, 0], here.at[d, 0], left),
        )

    def same(d, dev):
        return start(full_ref.at[d], full_ref.at[d], dev)

    def same_half(d, h, dev):
        return start(full_ref.at[d, h], full_ref.at[d, h], dev)

    z_in = {k: same(mine, along[k]) for k in (1, 2, 3)}
    rings = {0: ring(mine)}
    twins = [same(mine, twin)]
    zb = [rem4(zl + 4 - k) for k in range(4)]

    out_ref[...] = (preact * sig).astype(BF16)
    term_ref[:, 0:256] = lax.dot_general(
        aggregate, grad_pre, (((0,), (0,)), ((), ())), preferred_element_type=F32
    )
    term_ref[:, 256:384] = lax.dot_general(
        grad_pre, jnp.ones((256, 128), BF16), (((0,), (0,)), ((), ())), preferred_element_type=F32
    )

    forwards = {}

    def relay(k):
        dl, dr = at(xk[3], zb[k]), at(xk[1], zb[k])
        rings[k][0].wait_recv()
        fr = same_half(dl, 0, right)
        rings[k][1].wait_recv()
        fl = same_half(dr, 1, left)
        forwards[k] = (fr, fl)

    def hand_over(k):
        dl, dr = at(xk[3], zb[k]), at(xk[1], zb[k])
        rings[k][2].wait_recv()
        twins.append(same(dl, twin))
        rings[k][3].wait_recv()
        twins.append(same(dr, twin))

    for k in range(4):
        if k < 3:
            d = at(x, zb[k + 1])
            z_in[k + 1].wait_recv()
            rings[k + 1] = ring(d)
            twins.append(same(d, twin))
        relay(k)
        hand_over(k)
    for k in range(4):
        d = at(xk[2], zb[k])
        forwards[k][0].wait_recv()
        twins.append(same_half(d, 0, twin))
        forwards[k][1].wait_recv()
        twins.append(same_half(d, 1, twin))
    for c in twins:
        c.wait_recv()
    for c in started:
        c.wait_send()


def middle(part, cot, weight, bias):
    vmem = pl.BlockSpec(memory_space=pltpu.VMEM)
    chunk = (256, 256)
    return pl.pallas_call(
        middle_kernel,
        out_shape=(
            jax.ShapeDtypeStruct(chunk, BF16),
            jax.ShapeDtypeStruct((32, 2, 256, 128), BF16),
            jax.ShapeDtypeStruct((256, 384), F32),
        ),
        in_specs=[vmem] * 4,
        out_specs=(vmem,) * 3,
        scratch_shapes=[
            pltpu.VMEM((16,) + chunk, BF16),
            pltpu.VMEM((16,) + chunk, BF16),
            pltpu.VMEM((4, 128, 256), BF16),
            pltpu.VMEM((4, 128, 256), BF16),
            pltpu.VMEM((4,) + chunk, BF16),
            pltpu.VMEM((4,) + chunk, BF16),
            pltpu.VMEM((4,) + chunk, BF16),
            pltpu.VMEM((4,) + chunk, BF16),
            pltpu.SemaphoreType.DMA((96,)),
            pltpu.SemaphoreType.DMA((96,)),
        ],
        compiler_params=pltpu.CompilerParams(
            collective_id=1, has_side_effects=True, vmem_limit_bytes=VMEM_LIMIT
        ),
        name="layer",
    )(part, cot, weight, bias)


def backward_kernel(rows, cols, live, a_ref, g_ref, out_ref, acc):
    g = pl.program_id(0)
    n_cb = acc.shape[0] - 1

    @pl.when(g == 0)
    def _():
        def clear(i, _):
            acc[i] = jnp.zeros(acc.shape[1:], F32)
            return 0

        lax.fori_loop(0, n_cb, clear, 0)

    count = jnp.clip(live[0] - g * GROUP, 0, GROUP)

    def some(q, _):
        products = []
        for u in range(UNROLL):
            s = q * UNROLL + u
            products.append(
                jnp.dot(g_ref[rows[g * GROUP + s]], a_ref[s], preferred_element_type=F32)
            )
        for u in range(UNROLL):
            s = g * GROUP + q * UNROLL + u
            c = jnp.where(s < live[0], cols[s], n_cb)
            acc[c] += products[u]
        return 0

    lax.fori_loop(0, (count + UNROLL - 1) // UNROLL, some, 0)

    @pl.when(g == pl.num_programs(0) - 1)
    def _():
        for c in range(n_cb):
            out_ref[:, c * 128 : (c + 1) * 128] = acc[c].astype(BF16)


def backward_products(rows, cols, live, blocks, grads):
    n_slots = blocks.shape[0]
    return pl.pallas_call(
        backward_kernel,
        out_shape=jax.ShapeDtypeStruct((256, 2048), BF16),
        grid_spec=pltpu.PrefetchScalarGridSpec(
            num_scalar_prefetch=3,
            grid=(n_slots // GROUP,),
            in_specs=[
                pl.BlockSpec((GROUP, 128, 128), lambda g, *_: (g, 0, 0)),
                pl.BlockSpec((64, 256, 128), lambda g, *_: (0, 0, 0)),
            ],
            out_specs=pl.BlockSpec((256, 2048), lambda g, *_: (0, 0)),
            scratch_shapes=[pltpu.VMEM((17, 256, 128), F32)],
        ),
        compiler_params=pltpu.CompilerParams(vmem_limit_bytes=VMEM_LIMIT),
        name="backward_products",
    )(rows, cols, live, blocks, grads)


def finish_kernel(
    norm, part, term_ref, gx_ref, gw_ref, gb_ref,
    r_b1l, r_b1r, s_b1r, s_b1l, r_b2l, r_b2r, s_b, r_c,
    t_c, u_c, t_x, u_x, t_y, u_y, t_z, all_t, sends, recvs,
):
    zh, y, x, zl, core = place()
    right = device(zh, rem4(y + 1), x, zl, core)
    left = device(zh, rem4(y + 3), x, zl, core)
    across = device(1 - zh, y, x, zl, core)
    twin = device(zh, y, x, zl, 1 - core)
    y_dev = [None] + [device(zh, rem4(y + k), x, zl, core) for k in range(1, 4)]
    x_dev = [None] + [device(zh, y, rem4(x + k), zl, core) for k in range(1, 4)]
    zz = zh * 4 + zl
    z_dev = [None]
    for k in range(1, 8):
        other = lax.rem(zz + k, 8)
        z_dev.append(device(other // 4, y, x, lax.rem(other, 4), core))
    meet([twin] + y_dev[1:] + x_dev[1:] + z_dev[1:])
    started = []
    used = [0]

    def start(src, dst, dev):
        c = copy_to(src, dst, sends, recvs, used[0], dev)
        used[0] += 1
        c.start()
        started.append(c)
        return c

    yk = [rem4(y + k) for k in range(4)]
    xk = [rem4(x + k) for k in range(4)]
    top, low = pl.ds(0, 16), pl.ds(16, 16)

    def parameters():
        half = pl.ds(pl.multiple_of(core * 128, 128), 128)
        c = start(term_ref.at[pl.ds(pl.multiple_of((1 - core) * 128, 128), 128)], t_c, twin)
        yield
        c.wait_recv()
        u_c[...] = term_ref[half] + t_c[...]
        cs = [
            start(u_c.at[pl.ds(pl.multiple_of(xk[k] * 32, 32), 32)], t_x.at[k], x_dev[k])
            for k in (2, 1, 3)
        ]
        yield
        for c in cs:
            c.wait_recv()
        u_x[...] = u_c[pl.ds(pl.multiple_of(x * 32, 32), 32)] + (t_x[1] + t_x[2] + t_x[3])
        cs = [
            start(u_x.at[pl.ds(pl.multiple_of(yk[k] * 8, 8), 8)], t_y.at[k], y_dev[k])
            for k in (2, 1, 3)
        ]
        yield
        for c in cs:
            c.wait_recv()
        u_y[...] = u_x[pl.ds(pl.multiple_of(y * 8, 8), 8)] + (t_y[1] + t_y[2] + t_y[3])
        cs = [start(u_y, t_z.at[zz], z_dev[k]) for k in (4, 3, 5, 2, 6, 1, 7)]
        t_z[zz] = u_y[...]
        yield
        for c in cs:
            c.wait_recv()
        value = t_z[0]
        for k in range(1, 8):
            value = value + t_z[k]
        spot = pl.ds(pl.multiple_of(core * 128 + x * 32 + y * 8, 8), 8)
        all_t[spot] = value * norm
        cs = [start(all_t.at[spot], all_t.at[spot], y_dev[k]) for k in (2, 1, 3)]
        yield
        for c in cs:
            c.wait_recv()
        spot = pl.ds(pl.multiple_of(core * 128 + x * 32, 32), 32)
        cs = [start(all_t.at[spot], all_t.at[spot], x_dev[k]) for k in (2, 1, 3)]
        yield
        for c in cs:
            c.wait_recv()
        c = start(all_t.at[half], all_t.at[half], twin)
        yield
        c.wait_recv()
        gw_ref[...] = all_t[:, 0:256]
        gb_ref[...] = all_t[:, 256:384]
        yield

    params = parameters()
    next(params)
    zs = (1 - zh, zh)
    b1, b2 = [], []
    for j in range(2):
        i = zs[j] * 4 + yk[2]
        b1.append(
            (start(part.at[i, top], r_b1l.at[j], right), start(part.at[i, low], r_b1r.at[j], left))
        )
        b2.append(
            [
                start(part.at[zs[j] * 4 + yk[1], low], r_b2l.at[j, low], right),
                start(part.at[zs[j] * 4 + yk[3], top], r_b2r.at[j, top], left),
            ]
        )
    next(params)
    for j in range(2):
        b1[j][0].wait_recv()
        s_b1r[j] = (part[zs[j] * 4 + yk[1], top].astype(F32) + r_b1l[j].astype(F32)).astype(BF16)
        b2[j].append(start(s_b1r.at[j], r_b2l.at[j, top], right))
        b1[j][1].wait_recv()
        s_b1l[j] = (part[zs[j] * 4 + yk[3], low].astype(F32) + r_b1r[j].astype(F32)).astype(BF16)
        b2[j].append(start(s_b1l.at[j], r_b2r.at[j, low], left))
    next(params)

    def summed(j):
        for c in b2[j]:
            c.wait_recv()
        return part[zs[j] * 4 + y].astype(F32) + (r_b2l[j].astype(F32) + r_b2r[j].astype(F32))

    s_b[...] = summed(0).astype(BF16)
    cz = start(s_b, r_c, across)
    next(params)
    own = summed(1)
    cz.wait_recv()
    gx_ref[...] = (own + r_c[...].astype(F32)).astype(BF16)
    for _ in params:
        pass
    for c in started:
        c.wait_send()


def finish(part, term, norm):
    vmem = pl.BlockSpec(memory_space=pltpu.VMEM)
    half, whole = (2, 16, 2048), (2, 32, 2048)
    return pl.pallas_call(
        functools.partial(finish_kernel, norm),
        out_shape=(
            jax.ShapeDtypeStruct((32, 2048), BF16),
            jax.ShapeDtypeStruct((256, 256), F32),
            jax.ShapeDtypeStruct((256, 128), F32),
        ),
        in_specs=[vmem] * 2,
        out_specs=(vmem,) * 3,
        scratch_shapes=[
            pltpu.VMEM(half, BF16),
            pltpu.VMEM(half, BF16),
            pltpu.VMEM(half, BF16),
            pltpu.VMEM(half, BF16),
            pltpu.VMEM(whole, BF16),
            pltpu.VMEM(whole, BF16),
            pltpu.VMEM(whole[1:], BF16),
            pltpu.VMEM(whole[1:], BF16),
            pltpu.VMEM((128, 384), F32),
            pltpu.VMEM((128, 384), F32),
            pltpu.VMEM((4, 32, 384), F32),
            pltpu.VMEM((32, 384), F32),
            pltpu.VMEM((4, 8, 384), F32),
            pltpu.VMEM((8, 384), F32),
            pltpu.VMEM((8, 8, 384), F32),
            pltpu.VMEM((256, 384), F32),
            pltpu.SemaphoreType.DMA((40,)),
            pltpu.SemaphoreType.DMA((40,)),
        ],
        compiler_params=pltpu.CompilerParams(
            collective_id=2, has_side_effects=True, vmem_limit_bytes=VMEM_LIMIT
        ),
        name="finish",
    )(part, term)


def on_device(features, block_values, block_coords, live_blocks, weight, bias, cotangent):
    blocks = block_values[0, 0]
    rows, cols = block_coords[0, 0, 0], block_coords[0, 0, 1]
    live = live_blocks[0]
    nodes = features.shape[0] * lax.axis_size("col")
    x_t = gather_rows(features.T).reshape(256, 2048)
    part = forward_products(rows, cols, live, blocks, x_t)
    out, grads, term = middle(part, cotangent, weight, bias[None])
    part_x = backward_products(rows, cols, live, blocks, grads.reshape(64, 256, 128))
    gx_t, grad_weight, grad_bias = finish(part_x.reshape(8, 32, 2048), term, nodes**-0.5)
    return out, gx_t.T, grad_weight, grad_bias[:, 0]


def solution(mesh):
    in_specs = (
        P("col", "row"),
        P("row", "col", None, None, None),
        P("row", "col", None, None),
        P("row", "col"),
        P(),
        P(),
        P(("row", "col"), None),
    )
    out_specs = (P(("row", "col"), None), P("col", "row"), P(), P())
    return jax.shard_map(
        on_device, mesh=mesh, in_specs=in_specs, out_specs=out_specs, check_vma=False
    )
```

time: 786 us -> 174 us (0.22)
  waiting for transfers between devices: 441 us -> 0 us
  Pallas kernels: 0 us -> 165 us
  other arithmetic: 139 us -> 0 us
  blocking collectives: 76.7 us -> 0 us
  matrix products: 62.7 us -> 0 us
  local copies, waits for them, and re-layouts: 51.4 us -> 6.8 us
  between operations: 13.8 us -> 1.31 us
    reduce_scatter x2 -> x0, waiting for transfers between devices: 252 us -> none  [the longest x1 156 us: on_device(): lax.psum_scatter(partial_value, 'col', scatter_dimension=0, tiled=True)]
    pallas_call x0 -> x5, Pallas kernels: none -> 165 us  [the longest x1 73.6 us: middle(): pl.pallas_call(middle_kernel, out_shape=(jax.ShapeDtypeStruct(chunk, BF16...]
    scatter-add x8 -> x0, other arithmetic: 128 us -> none  [one_group(): return totals.at[put_to].add(products)]
    all_gather x2 -> x0, waiting for transfers between devices: 116 us -> none  [the longest x1 66.2 us: on_device(): feat_tile = lax.all_gather(features, 'row', axis=1, tiled=True)]
    psum x1 -> x0, blocking collectives: 76.7 us -> none  [on_device(): weight_sum, bias_sum = lax.psum((weight_term, bias_term), ('row', 'col'))]
    psum x1 -> x0, waiting for transfers between devices: 71.5 us -> none  [on_device(): weight_sum, bias_sum = lax.psum((weight_term, bias_term), ('row', 'col'))]
    dot_general x11 -> x0, matrix products: 62.7 us -> none  [the longest x8 59 us: one_group(): jnp.einsum(pattern, slab_vals, picked, preferred_element_type=jnp.float32)]
    gather x8 -> x0, local copies, waits for them, and re-layouts: 30.9 us -> none  [one_group(): picked = jnp.take(source, take_from, axis=0)]
  transfers between devices with their start and end apart: 5 -> 0, of which waited for: 5 -> 0; matrix products, arithmetic and copies ran while one was open for 15% -> 0% of each run, Pallas kernels for 0% -> 0%
where the time goes in v1:
time: 174 us; the launch traced here: 173 us
  Pallas kernels  165 us (95%)
  local copies, waits for them, and re-layouts  6.8 us (4%)
    pallas_call x1, Pallas kernels, middle(): pl.pallas_call(middle_kernel, out_shape=(jax.ShapeDtypeStruct(chunk, BF16...  73.6 us
    pallas_call x1, Pallas kernels, finish(): pl.pallas_call(functools.partial(finish_kernel, norm), out_shape=(jax.Sha...  48.6 us
    pallas_call x1, Pallas kernels, gather_rows(): pl.pallas_call(gather_rows_kernel, out_shape=jax.ShapeDtypeStruct((8, wid...  20.7 us
    pallas_call x1, Pallas kernels, forward_products(): pl.pallas_call(forward_kernel, out_shape=jax.ShapeDtypeStruct((2, 16, 256...  11.6 us
    pallas_call x1, Pallas kernels, backward_products(): pl.pallas_call(backward_kernel, out_shape=jax.ShapeDtypeStruct((256, 2048...  10.8 us
    unnamed x5, local copies, waits for them, and re-layouts  3.89 us

profile of v1, /device:TPU:1, one launch (start us, length us, event | category | flops | bytes accessed | tf_op | source)
XLA Modules:
  0.0 173.4 jit_solution(2937007703984701794)
XLA Ops:
  1.3 1.3 fusion
  2.6 20.7 %gather_features.1 = bf16[8,32,2048]{2,1,0:T(8,128)(2,1)} custom-call(bf16[32,2048]{1,0:T(8,128)(2,1)} %bitcast.17), custom_call_target="tpu_custom_call" | custom-call | tf_op jit(solution)/shard_map/gather_features/pallas_call | solution.py:128
  23.3 11.6 %forward_products.1.part = bf16[2,16,256,256]{3,2,1,0:T(8,128)(2,1)} custom-call(s32[256]{0:T(256)} %bitcast.21, s32[256]{0:T(256)} %bitcast.19, s32[1]{0:T(128)} %bitcast.10.live, bf16[256,128,128]{2,1,0:T(8,128)(2,1)} %bitcast.12, bf16[256,2048]{1,0:T(8,128)(2,1)} %bitcast.16), custom_call_target="tpu_custom_call" | custom-call | tf_op jit(solution)/shard_map/forward_products/pallas_call | solution.py:186
  34.9 73.6 %layer.1 = (bf16[256,256]{1,0:T(8,128)(2,1)}, bf16[32,2,256,128]{3,2,1,0:T(8,128)(2,1)}, f32[256,384]{1,0:T(8,128)}) custom-call(bf16[2,16,256,256]{3,2,1,0:T(8,128)(2,1)} %forward_products.1.part, bf16[256,256]{1,0:T(8,128)(2,1)} %cot_ref.1, bf16[256,256]{1,0:T(8,128)(2,1)} %w_ref.1, f32[1,256]{1,0:T(1,128)} %bitcast.23), custom_call_target="tpu_custom_call" | custom-call | tf_op jit(solution)/shard_map/layer/pallas_call | solution.py:366
  108.5 0.0 copy-start
  108.5 10.8 %backward_products.1 = bf16[256,2048]{1,0:T(8,128)(2,1)} custom-call(s32[256]{0:T(256)} %bitcast.22, s32[256]{0:T(256)} %bitcast.20, s32[1]{0:T(128)} %bitcast.11.live, bf16[256,128,128]{2,1,0:T(8,128)(2,1)} %bitcast.13, bf16[64,256,128]{2,1,0:T(8,128)(2,1)} %bitcast.14), custom_call_target="tpu_custom_call" | custom-call | tf_op jit(solution)/shard_map/backward_products/pallas_call | solution.py:431
  119.3 48.6 %finish.1 = (bf16[32,2048]{1,0:T(8,128)(2,1)}, f32[256,256]{1,0:T(8,128)}, f32[256,128]{1,0:T(8,128)}) custom-call(bf16[8,32,2048]{2,1,0:T(8,128)(2,1)} %bitcast.15, f32[256,384]{1,0:T(8,128)} %get-tuple-element.12.term_ref), custom_call_target="tpu_custom_call" | custom-call | tf_op jit(solution)/shard_map/finish/pallas_call | solution.py:574
  167.9 1.6 slice_reduce_fusion
  169.5 0.0 copy-done
  169.5 0.7 copy.15
  170.1 1.6 copy.16
  171.7 1.7 copy.17
Async XLA Ops:
  108.5 61.0 %copy-start = (bf16[256,256]{1,0:T(8,128)(2,1)S(1)}, bf16[256,256]{1,0:T(8,128)(2,1)}, u32[]{:S(2)}) copy-start(bf16[256,256]{1,0:T(8,128)(2,1)} %get-tuple-element.22) | copy-start | bytes 393220

commit v2 on v1

v2 whole, which is shorter than its diff:
```python
import functools

import jax
import jax.numpy as jnp
from jax import lax
from jax.experimental import pallas as pl
from jax.experimental.pallas import tpu as pltpu
from jax.sharding import PartitionSpec as P

MESH = pl.DeviceIdType.MESH
F32 = jnp.float32
BF16 = jnp.bfloat16
UNROLL = 4
VMEM = pl.BlockSpec(memory_space=pltpu.VMEM)
SMEM = pl.BlockSpec(memory_space=pltpu.SMEM)
MIB = 2**20
GATHER_VMEM = 4 * MIB
FORWARD_VMEM = 24 * MIB
MIDDLE_VMEM = 24 * MIB
BACKWARD_VMEM = 20 * MIB
FINISH_VMEM = 6 * MIB


def place():
    row, col = lax.axis_index("row"), lax.axis_index("col")
    return row // 4, row % 4, col // 8, (col // 2) % 4, col % 2


def device(zh, y, x, zl, core):
    return (zh * 4 + y, (x * 4 + zl) * 2 + core)


def copy_to(src, dst, sends, recvs, at, dev):
    return pltpu.make_async_remote_copy(
        src_ref=src,
        dst_ref=dst,
        send_sem=sends.at[at],
        recv_sem=recvs.at[at],
        device_id=dev,
        device_id_type=MESH,
    )


def meet(devices):
    barrier = pltpu.get_barrier_semaphore()
    for dev in devices:
        pl.semaphore_signal(barrier, inc=1, device_id=dev, device_id_type=MESH)
    pl.semaphore_wait(barrier, len(devices))


def rem4(v):
    return lax.rem(v, 4)


def gather_rows_kernel(x_ref, full_ref, sends, recvs):
    zh, y, x, zl, core = place()
    right = device(zh, rem4(y + 1), x, zl, core)
    left = device(zh, rem4(y + 3), x, zl, core)
    across = device(1 - zh, y, x, zl, core)
    meet((left, right, across))
    mine = zh * 4 + y
    other = (1 - zh) * 4 + y
    halves = (pl.ds(0, 16), pl.ds(16, 16))
    started = []

    def start(c):
        c.start()
        started.append(c)
        return c

    zc = [
        start(copy_to(x_ref.at[h], full_ref.at[mine, h], sends, recvs, 12 + i, across))
        for i, h in enumerate(halves)
    ]
    full_ref[mine] = x_ref[...]
    firsts = []
    for k in range(2):
        me = mine if k == 0 else other
        base = (zh if k == 0 else 1 - zh) * 4
        src = x_ref if k == 0 else full_ref.at[other]

        def ring(h, at, dev):
            return start(
                copy_to(src.at[halves[h]], full_ref.at[me, halves[h]], sends, recvs, k * 6 + at, dev)
            )

        if k == 1:
            zc[0].wait_recv()
        r0 = ring(0, 0, right)
        if k == 1:
            zc[1].wait_recv()
        l1 = ring(1, 1, left)
        r1 = ring(1, 2, right)
        l0 = ring(0, 3, left)
        firsts.append((r0, l1, r1, l0, base))
        if k == 0:
            continue
    forwards = []
    for k in range(2):
        r0, l1, r1, l0, base = firsts[k]
        from_left = base + rem4(y + 3)
        from_right = base + rem4(y + 1)
        r0.wait_recv()
        fr = start(
            copy_to(
                full_ref.at[from_left, halves[0]],
                full_ref.at[from_left, halves[0]],
                sends,
                recvs,
                k * 6 + 4,
                right,
            )
        )
        l1.wait_recv()
        fl = start(
            copy_to(
                full_ref.at[from_right, halves[1]],
                full_ref.at[from_right, halves[1]],
                sends,
                recvs,
                k * 6 + 5,
                left,
            )
        )
        forwards += [r1, l0, fr, fl]
    for c in forwards:
        c.wait_recv()
    for c in started:
        c.wait_send()


def gather_rows(x_t):
    width, verts = x_t.shape
    return pl.pallas_call(
        gather_rows_kernel,
        out_shape=jax.ShapeDtypeStruct((8, width, verts), BF16),
        in_specs=[pl.BlockSpec(memory_space=pltpu.VMEM)],
        out_specs=pl.BlockSpec(memory_space=pltpu.VMEM),
        scratch_shapes=[pltpu.SemaphoreType.DMA((14,)), pltpu.SemaphoreType.DMA((14,))],
        compiler_params=pltpu.CompilerParams(
            collective_id=0, has_side_effects=True, vmem_limit_bytes=GATHER_VMEM
        ),
        name="gather_features",
    )(x_t)


def forward_kernel(coords, live, a_ref, xt_ref, out_ref, xs, acc):
    n_rb = acc.shape[0] - 1
    n_cb = xs.shape[0]
    for c in range(n_cb):
        xs[c] = xt_ref[:, c * 128 : (c + 1) * 128].T

    def clear(i, _):
        acc[i] = jnp.zeros(acc.shape[1:], F32)
        return 0

    lax.fori_loop(0, n_rb, clear, 0)

    def some(q, _):
        products = []
        for u in range(UNROLL):
            s = q * UNROLL + u
            products.append(jnp.dot(a_ref[s], xs[coords[1, s]], preferred_element_type=F32))
        for u in range(UNROLL):
            s = q * UNROLL + u
            r = jnp.where(s < live[0, 0], coords[0, s], n_rb)
            acc[r] += products[u]
        return 0

    lax.fori_loop(0, (live[0, 0] + UNROLL - 1) // UNROLL, some, 0)

    def put(chip, _):
        for k in range(4):
            out_ref[k // 2, chip, (k % 2) * 128 : (k % 2 + 1) * 128, :] = acc[chip * 4 + k].astype(BF16)
        return 0

    lax.fori_loop(0, 16, put, 0)


def forward_products(coords, live, blocks, x_t):
    return pl.pallas_call(
        forward_kernel,
        out_shape=jax.ShapeDtypeStruct((2, 16, 256, 256), BF16),
        in_specs=[SMEM, SMEM, VMEM, VMEM],
        out_specs=VMEM,
        scratch_shapes=[pltpu.VMEM((16, 128, 256), BF16), pltpu.VMEM((65, 128, 256), F32)],
        compiler_params=pltpu.CompilerParams(vmem_limit_bytes=FORWARD_VMEM),
        name="forward_products",
    )(coords, live, blocks, x_t)


def middle_kernel(
    norm, part, cot_ref, w_ref, bias_ref, out_ref, full_ref, all_t,
    r_a, s_a, r_b1l, r_b1r, r_b2l, r_b2r, s_b, r_c,
    term_ref, t_c, u_c, t_y, u_y, t_x, u_x, t_z, sends, recvs,
):
    zh, y, x, zl, core = place()
    right = device(zh, y, rem4(x + 1), zl, core)
    left = device(zh, y, rem4(x + 3), zl, core)
    twin = device(zh, y, x, zl, 1 - core)
    along = [None] + [device(zh, y, x, rem4(zl + k), core) for k in range(1, 4)]
    y_dev = [None] + [device(zh, rem4(y + k), x, zl, core) for k in range(1, 4)]
    x_dev = [None] + [device(zh, y, rem4(x + k), zl, core) for k in range(1, 4)]
    zz = zh * 4 + zl
    z_dev = [None]
    for k in range(1, 8):
        other = lax.rem(zz + k, 8)
        z_dev.append(device(other // 4, y, x, lax.rem(other, 4), core))
    meet([twin] + y_dev[1:] + x_dev[1:] + z_dev[1:])
    started = []
    used = [0]

    def start(src, dst, dev):
        c = copy_to(src, dst, sends, recvs, used[0], dev)
        used[0] += 1
        c.start()
        started.append(c)
        return c

    top, low = pl.ds(0, 128), pl.ds(128, 128)
    xk = [rem4(x + k) for k in range(4)]
    zk = [rem4(zl + k) for k in range(4)]
    order = (1, 2, 3, 0)
    a = {}
    for k in (2, 1, 3, 0):
        sl = pl.ds(xk[k] * 4, 4)
        a[k] = start(part.at[1 - core, sl], r_a.at[sl], twin)

    def add_cores(k):
        a[k].wait_recv()

        def one(z, _):
            i = xk[k] * 4 + z
            s_a[i] = (part[core, i].astype(F32) + r_a[i].astype(F32)).astype(BF16)
            return 0

        lax.fori_loop(0, 4, one, 0)

    add_cores(2)
    b1 = {}
    for k in order:
        i = xk[2] * 4 + zk[k]
        b1[k] = (
            start(s_a.at[i, top], r_b1l.at[k], right),
            start(s_a.at[i, low], r_b1r.at[k], left),
        )
    b2 = {}
    add_cores(1)
    for k in order:
        b2[k] = [start(s_a.at[xk[1] * 4 + zk[k], low], r_b2l.at[k, low], right)]
    add_cores(3)
    for k in order:
        b2[k].append(start(s_a.at[xk[3] * 4 + zk[k], top], r_b2r.at[k, top], left))
    for k in order:
        b1[k][0].wait_recv()
        i = xk[1] * 4 + zk[k]
        s_a[i, top] = (s_a[i, top].astype(F32) + r_b1l[k].astype(F32)).astype(BF16)
        b2[k].append(start(s_a.at[i, top], r_b2l.at[k, top], right))
        b1[k][1].wait_recv()
        j = xk[3] * 4 + zk[k]
        s_a[j, low] = (s_a[j, low].astype(F32) + r_b1r[k].astype(F32)).astype(BF16)
        b2[k].append(start(s_a.at[j, low], r_b2r.at[k, low], left))
    add_cores(0)
    c_z = {}
    total = None
    for k in order:
        for c in b2[k]:
            c.wait_recv()
        i = x * 4 + zk[k]
        value = s_a[i].astype(F32) + (r_b2l[k].astype(F32) + r_b2r[k].astype(F32))
        if k == 0:
            total = value
        else:
            s_b[k] = value.astype(BF16)
            c_z[k] = start(s_b.at[k], r_c.at[k], along[k])
    for k in (1, 2, 3):
        c_z[k].wait_recv()
        total = total + r_c[k].astype(F32)
    aggregate = total.astype(BF16)
    preact = jnp.dot(aggregate, w_ref[...], preferred_element_type=F32) + bias_ref[...]
    sig = jax.nn.sigmoid(preact)
    derivative = sig * (1.0 + preact * (1.0 - sig))
    grad_pre = (cot_ref[...].astype(F32) * derivative).astype(BF16)
    grad_agg = lax.dot_general(
        w_ref[...], grad_pre, (((1,), (1,)), ((), ())), preferred_element_type=F32
    ).astype(BF16)
    mine = (x * 4 + zl) * 2 + core
    full_ref[mine, 0] = grad_agg[:, 0:128]
    full_ref[mine, 1] = grad_agg[:, 128:256]

    def at(xx, zz):
        return (xx * 4 + zz) * 2 + core

    def ring(d):
        here = full_ref
        return (
            start(here.at[d, 0], here.at[d, 0], right),
            start(here.at[d, 1], here.at[d, 1], left),
            start(here.at[d, 1], here.at[d, 1], right),
            start(here.at[d, 0], here.at[d, 0], left),
        )

    def same(d, dev):
        return start(full_ref.at[d], full_ref.at[d], dev)

    def same_half(d, h, dev):
        return start(full_ref.at[d, h], full_ref.at[d, h], dev)

    z_in = {k: same(mine, along[k]) for k in (1, 2, 3)}
    rings = {0: ring(mine)}
    twins = [same(mine, twin)]
    zb = [rem4(zl + 4 - k) for k in range(4)]

    out_ref[...] = (preact * sig).astype(BF16)
    term_ref[:, 0:256] = lax.dot_general(
        aggregate, grad_pre, (((0,), (0,)), ((), ())), preferred_element_type=F32
    )
    term_ref[:, 256:384] = lax.dot_general(
        grad_pre, jnp.ones((256, 128), BF16), (((0,), (0,)), ((), ())), preferred_element_type=F32
    )

    yk = [rem4(y + k) for k in range(4)]

    def parameters():
        def at_row(row, n):
            return pl.ds(pl.multiple_of(row, n), n)

        half = at_row(core * 128, 128)
        c = start(term_ref.at[at_row((1 - core) * 128, 128)], t_c, twin)
        yield
        c.wait_recv()
        u_c[...] = term_ref[half] + t_c[...]
        cs = [start(u_c.at[at_row(yk[k] * 32, 32)], t_y.at[k], y_dev[k]) for k in (2, 1, 3)]
        yield
        for c in cs:
            c.wait_recv()
        u_y[...] = u_c[at_row(y * 32, 32)] + (t_y[1] + t_y[2] + t_y[3])
        cs = [start(u_y.at[at_row(xk[k] * 8, 8)], t_x.at[k], x_dev[k]) for k in (2, 1, 3)]
        yield
        for c in cs:
            c.wait_recv()
        u_x[...] = u_y[at_row(x * 8, 8)] + (t_x[1] + t_x[2] + t_x[3])
        cs = [start(u_x, t_z.at[zz], z_dev[k]) for k in (4, 3, 5, 2, 6, 1, 7)]
        t_z[zz] = u_x[...]
        yield
        for c in cs:
            c.wait_recv()
        value = t_z[0]
        for k in range(1, 8):
            value = value + t_z[k]
        spot = at_row(core * 128 + y * 32 + x * 8, 8)
        all_t[spot] = value * norm
        cs = [start(all_t.at[spot], all_t.at[spot], x_dev[k]) for k in (2, 1, 3)]
        yield
        for c in cs:
            c.wait_recv()
        spot = at_row(core * 128 + y * 32, 32)
        cs = [start(all_t.at[spot], all_t.at[spot], y_dev[k]) for k in (2, 1, 3)]
        yield
        for c in cs:
            c.wait_recv()
        c = start(all_t.at[half], all_t.at[half], twin)
        yield
        c.wait_recv()
        yield

    params = parameters()
    next(params)
    forwards = {}

    def relay(k):
        dl, dr = at(xk[3], zb[k]), at(xk[1], zb[k])
        rings[k][0].wait_recv()
        fr = same_half(dl, 0, right)
        rings[k][1].wait_recv()
        fl = same_half(dr, 1, left)
        forwards[k] = (fr, fl)

    def hand_over(k):
        dl, dr = at(xk[3], zb[k]), at(xk[1], zb[k])
        rings[k][2].wait_recv()
        twins.append(same(dl, twin))
        rings[k][3].wait_recv()
        twins.append(same(dr, twin))

    for k in range(4):
        if k < 3:
            d = at(x, zb[k + 1])
            z_in[k + 1].wait_recv()
            rings[k + 1] = ring(d)
            twins.append(same(d, twin))
        relay(k)
        if k > 0:
            next(params)
        hand_over(k)
        next(params)
    for k in range(4):
        d = at(xk[2], zb[k])
        forwards[k][0].wait_recv()
        twins.append(same_half(d, 0, twin))
        forwards[k][1].wait_recv()
        twins.append(same_half(d, 1, twin))
    for _ in params:
        pass
    for c in twins:
        c.wait_recv()
    for c in started:
        c.wait_send()


def middle(part, cot, weight, bias, norm):
    chunk = (256, 256)
    return pl.pallas_call(
        functools.partial(middle_kernel, norm),
        out_shape=(
            jax.ShapeDtypeStruct(chunk, BF16),
            jax.ShapeDtypeStruct((32, 2, 256, 128), BF16),
            jax.ShapeDtypeStruct((256, 384), F32),
        ),
        in_specs=[VMEM] * 4,
        out_specs=(VMEM,) * 3,
        scratch_shapes=[
            pltpu.VMEM((16,) + chunk, BF16),
            pltpu.VMEM((16,) + chunk, BF16),
            pltpu.VMEM((4, 128, 256), BF16),
            pltpu.VMEM((4, 128, 256), BF16),
            pltpu.VMEM((4,) + chunk, BF16),
            pltpu.VMEM((4,) + chunk, BF16),
            pltpu.VMEM((4,) + chunk, BF16),
            pltpu.VMEM((4,) + chunk, BF16),
            pltpu.VMEM((256, 384), F32),
            pltpu.VMEM((128, 384), F32),
            pltpu.VMEM((128, 384), F32),
            pltpu.VMEM((4, 32, 384), F32),
            pltpu.VMEM((32, 384), F32),
            pltpu.VMEM((4, 8, 384), F32),
            pltpu.VMEM((8, 384), F32),
            pltpu.VMEM((8, 8, 384), F32),
            pltpu.SemaphoreType.DMA((112,)),
            pltpu.SemaphoreType.DMA((112,)),
        ],
        compiler_params=pltpu.CompilerParams(
            collective_id=1, has_side_effects=True, vmem_limit_bytes=MIDDLE_VMEM
        ),
        name="layer",
    )(part, cot, weight, bias)


def backward_kernel(coords, live, a_ref, g_ref, o_ref, t_ref, out_ref, o_out, gw_out, gb_out, acc):
    n_cb = acc.shape[0] - 1
    o_out[...] = o_ref[...]
    gw_out[...] = t_ref[:, 0:256]
    gb_out[...] = t_ref[:, 256:384].T[0:1]

    def clear(i, _):
        acc[i] = jnp.zeros(acc.shape[1:], F32)
        return 0

    lax.fori_loop(0, n_cb, clear, 0)

    def some(q, _):
        products = []
        for u in range(UNROLL):
            s = q * UNROLL + u
            products.append(jnp.dot(g_ref[coords[0, s]], a_ref[s], preferred_element_type=F32))
        for u in range(UNROLL):
            s = q * UNROLL + u
            c = jnp.where(s < live[0, 0], coords[1, s], n_cb)
            acc[c] += products[u]
        return 0

    lax.fori_loop(0, (live[0, 0] + UNROLL - 1) // UNROLL, some, 0)
    for c in range(n_cb):
        out_ref[:, c * 128 : (c + 1) * 128] = acc[c].astype(BF16)


def backward_products(coords, live, blocks, grads, out, term):
    return pl.pallas_call(
        backward_kernel,
        out_shape=(
            jax.ShapeDtypeStruct((256, 2048), BF16),
            jax.ShapeDtypeStruct((256, 256), BF16),
            jax.ShapeDtypeStruct((256, 256), F32),
            jax.ShapeDtypeStruct((1, 256), F32),
        ),
        in_specs=[SMEM, SMEM, VMEM, VMEM, VMEM, VMEM],
        out_specs=(VMEM,) * 4,
        scratch_shapes=[pltpu.VMEM((17, 256, 128), F32)],
        compiler_params=pltpu.CompilerParams(vmem_limit_bytes=BACKWARD_VMEM),
        name="backward_products",
    )(coords, live, blocks, grads, out, term)


def finish_kernel(
    part, gx_ref, r_b1l, r_b1r, s_b1r, s_b1l, r_b2l, r_b2r, s_b, r_c, sends, recvs,
):
    zh, y, x, zl, core = place()
    right = device(zh, rem4(y + 1), x, zl, core)
    left = device(zh, rem4(y + 3), x, zl, core)
    across = device(1 - zh, y, x, zl, core)
    meet((left, right, across))
    started = []
    used = [0]

    def start(src, dst, dev):
        c = copy_to(src, dst, sends, recvs, used[0], dev)
        used[0] += 1
        c.start()
        started.append(c)
        return c

    yk = [rem4(y + k) for k in range(4)]
    top, low = pl.ds(0, 16), pl.ds(16, 16)

    zs = (1 - zh, zh)
    b1, b2 = [], []

    def first(j):
        i = zs[j] * 4 + yk[2]
        b1.append(
            (start(part.at[i, top], r_b1l.at[j], right), start(part.at[i, low], r_b1r.at[j], left))
        )

    def plain(j):
        b2.append(
            [
                start(part.at[zs[j] * 4 + yk[1], low], r_b2l.at[j, low], right),
                start(part.at[zs[j] * 4 + yk[3], top], r_b2r.at[j, top], left),
            ]
        )

    def added(j):
        b1[j][0].wait_recv()
        s_b1r[j] = (part[zs[j] * 4 + yk[1], top].astype(F32) + r_b1l[j].astype(F32)).astype(BF16)
        b2[j].append(start(s_b1r.at[j], r_b2l.at[j, top], right))
        b1[j][1].wait_recv()
        s_b1l[j] = (part[zs[j] * 4 + yk[3], low].astype(F32) + r_b1r[j].astype(F32)).astype(BF16)
        b2[j].append(start(s_b1l.at[j], r_b2r.at[j, low], left))

    first(0)
    plain(0)
    first(1)
    added(0)
    plain(1)
    added(1)

    def summed(j):
        for c in b2[j]:
            c.wait_recv()
        return part[zs[j] * 4 + y].astype(F32) + (r_b2l[j].astype(F32) + r_b2r[j].astype(F32))

    s_b[...] = summed(0).astype(BF16)
    cz = start(s_b, r_c, across)
    own = summed(1)
    cz.wait_recv()
    gx_ref[...] = (own + r_c[...].astype(F32)).astype(BF16)
    for c in started:
        c.wait_send()


def finish(part):
    half, whole = (2, 16, 2048), (2, 32, 2048)
    return pl.pallas_call(
        finish_kernel,
        out_shape=jax.ShapeDtypeStruct((32, 2048), BF16),
        in_specs=[VMEM],
        out_specs=VMEM,
        scratch_shapes=[
            pltpu.VMEM(half, BF16),
            pltpu.VMEM(half, BF16),
            pltpu.VMEM(half, BF16),
            pltpu.VMEM(half, BF16),
            pltpu.VMEM(whole, BF16),
            pltpu.VMEM(whole, BF16),
            pltpu.VMEM(whole[1:], BF16),
            pltpu.VMEM(whole[1:], BF16),
            pltpu.SemaphoreType.DMA((16,)),
            pltpu.SemaphoreType.DMA((16,)),
        ],
        compiler_params=pltpu.CompilerParams(
            collective_id=2, has_side_effects=True, vmem_limit_bytes=FINISH_VMEM
        ),
        name="finish",
    )(part)


def on_device(features, block_values, block_coords, live_blocks, weight, bias, cotangent):
    blocks, coords = block_values[0, 0], block_coords[0, 0]
    nodes = features.shape[0] * lax.axis_size("col")
    x_t = gather_rows(features.T).reshape(256, 2048)
    part = forward_products(coords, live_blocks, blocks, x_t)
    out, grads, term = middle(part, cotangent, weight, bias[None], nodes**-0.5)
    part_x, out, grad_weight, grad_bias = backward_products(
        coords, live_blocks, blocks, grads.reshape(64, 256, 128), out, term
    )
    gx_t = finish(part_x.reshape(8, 32, 2048))
    return out, gx_t.T, grad_weight, grad_bias[0]


def solution(mesh):
    in_specs = (
        P("col", "row"),
        P("row", "col", None, None, None),
        P("row", "col", None, None),
        P("row", "col"),
        P(),
        P(),
        P(("row", "col"), None),
    )
    out_specs = (P(("row", "col"), None), P("col", "row"), P(), P())
    return jax.shard_map(
        on_device, mesh=mesh, in_specs=in_specs, out_specs=out_specs, check_vma=False
    )
```

time: 174 us -> 154 us (0.89)
  Pallas kernels: 165 us -> 146 us
    pallas_call x3, Pallas kernels: 133 us -> 111 us  [the longest x1 79.4 us: middle(): pl.pallas_call(functools.partial(middle_kernel, norm), out_shape=(jax.Sha...]
    pallas_call x1, Pallas kernels: 11.6 us -> 16.8 us  [forward_products(): pl.pallas_call(forward_kernel, out_shape=jax.ShapeDtypeStruct((2, 16, 256...]
    slice x2 -> x0, local copies, waits for them, and re-layouts: 2.91 us -> none  [the longest x1 1.58 us: on_device(): return (out, gx_t.T, grad_weight, grad_bias[:, 0])]
    pallas_call x1, Pallas kernels: 20.7 us -> 18.8 us  [gather_rows(): pl.pallas_call(gather_rows_kernel, out_shape=jax.ShapeDtypeStruct((8, wid...]
    unnamed x5 -> x17, local copies, waits for them, and re-layouts: 3.89 us -> 5.63 us
where the time goes in v2:
time: 154 us; the launch traced here: 153 us
  Pallas kernels  146 us (95%)
  local copies, waits for them, and re-layouts  5.63 us (4%)
    pallas_call x1, Pallas kernels, middle(): pl.pallas_call(functools.partial(middle_kernel, norm), out_shape=(jax.Sha...  79.4 us
    pallas_call x1, Pallas kernels, gather_rows(): pl.pallas_call(gather_rows_kernel, out_shape=jax.ShapeDtypeStruct((8, wid...  18.8 us
    pallas_call x1, Pallas kernels, forward_products(): pl.pallas_call(forward_kernel, out_shape=jax.ShapeDtypeStruct((2, 16, 256...  16.8 us
    pallas_call x1, Pallas kernels, backward_products(): pl.pallas_call(backward_kernel, out_shape=(jax.ShapeDtypeStruct((256, 204...  16.1 us
    pallas_call x1, Pallas kernels, finish(): pl.pallas_call(finish_kernel, out_shape=jax.ShapeDtypeStruct((32, 2048),...  15.3 us
    unnamed x17, local copies, waits for them, and re-layouts  5.63 us

profile of v2, /device:TPU:1, one launch (start us, length us, event | category | flops | bytes accessed | tf_op | source)
XLA Modules:
  0.0 153.4 jit_solution(12376642712506549034)
XLA Ops:
  1.3 0.0 copy-start.2
  1.3 0.9 copy-done.2
  2.2 18.8 %gather_features.1 = bf16[8,32,2048]{2,1,0:T(8,128)(2,1)S(1)} custom-call(bf16[32,2048]{1,0:T(8,128)(2,1)S(1)} %bitcast.15), custom_call_target="tpu_custom_call" | custom-call | tf_op jit(solution)/shard_map/gather_features/pallas_call | solution.py:134
  21.0 0.0 copy-start
  21.0 3.4 %copy-done = bf16[1,1,256,128,128]{4,3,2,1,0:T(8,128)(2,1)S(1)} copy-done((bf16[1,1,256,128,128]{4,3,2,1,0:T(8,128)(2,1)S(1)}, bf16[1,1,256,128,128]{4,3,2,1,0:T(8,128)(2,1)}, u32[]{:S(2)}) %copy-start) | copy-done | bytes 8388632
  24.4 0.0 copy-start.5
  24.4 0.7 copy-done.5
  25.1 0.0 copy-start.3
  25.1 0.0 copy-start.4
  25.1 0.0 copy-start.7
  25.1 0.0 copy-start.1
  25.1 16.8 %forward_products.1.part = bf16[2,16,256,256]{3,2,1,0:T(8,128)(2,1)S(1)} custom-call(s32[2,256]{1,0:T(2,128)S(1)} %bitcast.16, s32[1,1]{1,0:T(1,128)S(6)} %copy.12.live, bf16[256,128,128]{2,1,0:T(8,128)(2,1)S(1)} %bitcast.9, bf16[256,2048]{1,0:T(8,128)(2,1)S(1)} %bitcast.11), custom_call_target="tpu_custom_call" | custom-call | tf_op jit(solution)/shard_map/forward_products/pallas_call | solution.py:181
  41.8 0.0 copy-done.3
  41.9 0.0 copy-done.4
  41.9 0.0 copy-done.7
  41.9 0.0 copy-start.6
  41.9 79.4 %layer.1 = (bf16[256,256]{1,0:T(8,128)(2,1)S(1)}, bf16[32,2,256,128]{3,2,1,0:T(8,128)(2,1)S(1)}, f32[256,384]{1,0:T(8,128)S(1)}) custom-call(bf16[2,16,256,256]{3,2,1,0:T(8,128)(2,1)S(1)} %forward_products.1.part, bf16[256,256]{1,0:T(8,128)(2,1)S(1)} %copy-done.3, bf16[256,256]{1,0:T(8,128)(2,1)S(1)} %copy-done.4, f32[1,256]{1,0:T(1,128)S(1)} %bitcast.18), custom_call_target="tpu_custom_call" | custom-call | tf_op jit(solution)/shard_map/layer/pallas_call | solution.py:413
  121.3 0.0 copy-done.1
  121.3 0.0 copy-done.6
  121.3 16.1 %backward_products.1 = (bf16[256,2048]{1,0:T(8,128)(2,1)S(1)}, bf16[256,256]{1,0:T(8,128)(2,1)}, f32[256,256]{1,0:T(8,128)}, f32[1,256]{1,0:T(1,128)}) custom-call(s32[2,256]{1,0:T(2,128)S(1)} %bitcast.17, s32[1,1]{1,0:T(1,128)S(6)} %copy.12.live, bf16[256,128,128]{2,1,0:T(8,128)(2,1)S(1)} %bitcast.10, bf16[64,256,128]{2,1,0:T(8,128)(2,1)S(1)} %bitcast.12, ...), custom_call_target="tpu_custom_call" | custom-call | tf_op jit(solution)/shard_map/backward_products/pallas_call | solution.py:478
  137.4 15.3 %finish.1 = bf16[32,2048]{1,0:T(8,128)(2,1)S(1)} custom-call(bf16[8,32,2048]{2,1,0:T(8,128)(2,1)S(1)} %bitcast.13), custom_call_target="tpu_custom_call" | custom-call | tf_op jit(solution)/shard_map/finish/pallas_call | solution.py:563
  152.7 0.7 copy.13
Async XLA Ops:
  1.3 0.9 copy-start.2
  21.0 3.4 %copy-start = (bf16[1,1,256,128,128]{4,3,2,1,0:T(8,128)(2,1)S(1)}, bf16[1,1,256,128,128]{4,3,2,1,0:T(8,128)(2,1)}, u32[]{:S(2)}) copy-start(bf16[1,1,256,128,128]{4,3,2,1,0:T(8,128)(2,1)} %param.8) | copy-start | bytes 25165828
  24.4 0.7 copy-start.5
  25.1 16.8 %copy-start.3 = (bf16[256,256]{1,0:T(8,128)(2,1)S(1)}, bf16[256,256]{1,0:T(8,128)(2,1)}, u32[]{:S(2)}) copy-start(bf16[256,256]{1,0:T(8,128)(2,1)} %cot_ref.1) | copy-start | bytes 393220
  25.1 16.8 %copy-start.4 = (bf16[256,256]{1,0:T(8,128)(2,1)S(1)}, bf16[256,256]{1,0:T(8,128)(2,1)}, u32[]{:S(2)}) copy-start(bf16[256,256]{1,0:T(8,128)(2,1)} %w_ref.1) | copy-start | bytes 393220
  25.1 16.8 %copy-start.7 = (f32[256]{0:T(256)S(1)}, f32[256]{0:T(256)}, u32[]{:S(2)}) copy-start(f32[256]{0:T(256)} %param.12) | copy-start | bytes 3076
  25.1 96.2 %copy-start.1 = (bf16[1,1,256,128,128]{4,3,2,1,0:T(8,128)(2,1)S(1)}, bf16[1,1,256,128,128]{4,3,2,1,0:T(8,128)(2,1)}, u32[]{:S(2)}) copy-start(bf16[1,1,256,128,128]{4,3,2,1,0:T(8,128)(2,1)} %param.8) | copy-start | bytes 25165828
  41.9 79.4 %copy-start.6 = (s32[1,1,2,256]{3,2,1,0:T(2,128)S(1)}, s32[1,1,2,256]{3,2,1,0:T(2,128)}, u32[]{:S(2)}) copy-start(s32[1,1,2,256]{3,2,1,0:T(2,128)} %param.9) | copy-start | bytes 6148

commit v3 on v2

--- a/solution.py
+++ b/solution.py
@@ -10,11 +10,12 @@
 MESH = pl.DeviceIdType.MESH
 F32 = jnp.float32
 BF16 = jnp.bfloat16
-UNROLL = 4
+UNROLL = 8
 VMEM = pl.BlockSpec(memory_space=pltpu.VMEM)
 SMEM = pl.BlockSpec(memory_space=pltpu.SMEM)
+ANY = pl.BlockSpec(memory_space=pltpu.HBM)
 MIB = 2**20
-GATHER_VMEM = 4 * MIB
+GATHER_VMEM = 42 * MIB
 FORWARD_VMEM = 24 * MIB
 MIDDLE_VMEM = 24 * MIB
 BACKWARD_VMEM = 20 * MIB
@@ -52,7 +53,7 @@
     return lax.rem(v, 4)
 
 
-def gather_rows_kernel(x_ref, full_ref, sends, recvs):
+def gather_rows_kernel(x_ref, b_ref, c_ref, full_ref, b_out, c_out, sends, recvs, locals_):
     zh, y, x, zl, core = place()
     right = device(zh, rem4(y + 1), x, zl, core)
     left = device(zh, rem4(y + 3), x, zl, core)
@@ -60,6 +61,10 @@
     meet((left, right, across))
     mine = zh * 4 + y
     other = (1 - zh) * 4 + y
+    staged = [
+        pltpu.make_async_copy(src, dst, locals_.at[i])
+        for i, (src, dst) in enumerate(((x_ref, full_ref.at[mine]), (b_ref, b_out), (c_ref, c_out)))
+    ]
     halves = (pl.ds(0, 16), pl.ds(16, 16))
     started = []
 
@@ -72,7 +77,6 @@
         start(copy_to(x_ref.at[h], full_ref.at[mine, h], sends, recvs, 12 + i, across))
         for i, h in enumerate(halves)
     ]
-    full_ref[mine] = x_ref[...]
     firsts = []
     for k in range(2):
         me = mine if k == 0 else other
@@ -94,7 +98,8 @@
         l0 = ring(0, 3, left)
         firsts.append((r0, l1, r1, l0, base))
         if k == 0:
-            continue
+            for c in staged:
+                c.start()
     forwards = []
     for k in range(2):
         r0, l1, r1, l0, base = firsts[k]
@@ -125,23 +130,33 @@
         forwards += [r1, l0, fr, fl]
     for c in forwards:
         c.wait_recv()
+    for c in staged:
+        c.wait()
     for c in started:
         c.wait_send()
 
 
-def gather_rows(x_t):
+def gather_rows(x_t, blocks, coords):
     width, verts = x_t.shape
     return pl.pallas_call(
         gather_rows_kernel,
-        out_shape=jax.ShapeDtypeStruct((8, width, verts), BF16),
-        in_specs=[pl.BlockSpec(memory_space=pltpu.VMEM)],
-        out_specs=pl.BlockSpec(memory_space=pltpu.VMEM),
-        scratch_shapes=[pltpu.SemaphoreType.DMA((14,)), pltpu.SemaphoreType.DMA((14,))],
+        out_shape=(
+            jax.ShapeDtypeStruct((8, width, verts), BF16),
+            jax.ShapeDtypeStruct(blocks.shape, BF16),
+            jax.ShapeDtypeStruct(coords.shape, jnp.int32),
+        ),
+        in_specs=[ANY] * 3,
+        out_specs=(VMEM,) * 3,
+        scratch_shapes=[
+            pltpu.SemaphoreType.DMA((14,)),
+            pltpu.SemaphoreType.DMA((14,)),
+            pltpu.SemaphoreType.DMA((3,)),
+        ],
         compiler_params=pltpu.CompilerParams(
             collective_id=0, has_side_effects=True, vmem_limit_bytes=GATHER_VMEM
         ),
         name="gather_features",
-    )(x_t)
+    )(x_t, blocks, coords)
 
 
 def forward_kernel(coords, live, a_ref, xt_ref, out_ref, xs, acc):
@@ -220,7 +235,7 @@
     top, low = pl.ds(0, 128), pl.ds(128, 128)
     xk = [rem4(x + k) for k in range(4)]
     zk = [rem4(zl + k) for k in range(4)]
-    order = (1, 2, 3, 0)
+    order = (2, 1, 3, 0)
     a = {}
     for k in (2, 1, 3, 0):
         sl = pl.ds(xk[k] * 4, 4)
@@ -236,22 +251,22 @@
 
         lax.fori_loop(0, 4, one, 0)
 
-    add_cores(2)
-    b1 = {}
-    for k in order:
+    b1, b2, c_z = {}, {}, {}
+
+    def first(k):
         i = xk[2] * 4 + zk[k]
         b1[k] = (
             start(s_a.at[i, top], r_b1l.at[k], right),
             start(s_a.at[i, low], r_b1r.at[k], left),
         )
-    b2 = {}
-    add_cores(1)
-    for k in order:
-        b2[k] = [start(s_a.at[xk[1] * 4 + zk[k], low], r_b2l.at[k, low], right)]
-    add_cores(3)
-    for k in order:
-        b2[k].append(start(s_a.at[xk[3] * 4 + zk[k], top], r_b2r.at[k, top], left))
-    for k in order:
+
+    def plain(k):
+        b2[k] = [
+            start(s_a.at[xk[1] * 4 + zk[k], low], r_b2l.at[k, low], right),
+            start(s_a.at[xk[3] * 4 + zk[k], top], r_b2r.at[k, top], left),
+        ]
+
+    def added(k):
         b1[k][0].wait_recv()
         i = xk[1] * 4 + zk[k]
         s_a[i, top] = (s_a[i, top].astype(F32) + r_b1l[k].astype(F32)).astype(BF16)
@@ -260,19 +275,34 @@
         j = xk[3] * 4 + zk[k]
         s_a[j, low] = (s_a[j, low].astype(F32) + r_b1r[k].astype(F32)).astype(BF16)
         b2[k].append(start(s_a.at[j, low], r_b2r.at[k, low], left))
-    add_cores(0)
-    c_z = {}
-    total = None
-    for k in order:
+
+    def summed(k):
         for c in b2[k]:
             c.wait_recv()
         i = x * 4 + zk[k]
-        value = s_a[i].astype(F32) + (r_b2l[k].astype(F32) + r_b2r[k].astype(F32))
-        if k == 0:
-            total = value
+        return s_a[i].astype(F32) + (r_b2l[k].astype(F32) + r_b2r[k].astype(F32))
+
+    def along_z(k):
+        s_b[k] = summed(k).astype(BF16)
+        c_z[k] = start(s_b.at[k], r_c.at[k], along[k])
+
+    add_cores(2)
+    first(order[0])
+    first(order[1])
+    add_cores(1)
+    add_cores(3)
+    plain(order[0])
+    for n in range(4):
+        added(order[n])
+        if n < 2:
+            first(order[n + 2])
+        if n < 3:
+            plain(order[n + 1])
+        if n == 0:
+            add_cores(0)
         else:
-            s_b[k] = value.astype(BF16)
-            c_z[k] = start(s_b.at[k], r_c.at[k], along[k])
+            along_z(order[n - 1])
+    total = summed(0)
     for k in (1, 2, 3):
         c_z[k].wait_recv()
         total = total + r_c[k].astype(F32)
@@ -384,17 +414,22 @@
         twins.append(same(dr, twin))
 
     for k in range(4):
+        relay(k)
+        if k == 1:
+            next(params)
+        hand_over(k)
+        if k > 0:
+            next(params)
         if k < 3:
             d = at(x, zb[k + 1])
             z_in[k + 1].wait_recv()
             rings[k + 1] = ring(d)
             twins.append(same(d, twin))
-        relay(k)
-        if k > 0:
+        if k == 0:
             next(params)
-        hand_over(k)
-        next(params)
     for k in range(4):
+        if k == 3:
+            next(params)
         d = at(xk[2], zb[k])
         forwards[k][0].wait_recv()
         twins.append(same_half(d, 0, twin))
@@ -537,12 +572,10 @@
         s_b1l[j] = (part[zs[j] * 4 + yk[3], low].astype(F32) + r_b1r[j].astype(F32)).astype(BF16)
         b2[j].append(start(s_b1l.at[j], r_b2r.at[j, low], left))
 
-    first(0)
-    plain(0)
-    first(1)
-    added(0)
-    plain(1)
-    added(1)
+    for j in range(2):
+        first(j)
+        plain(j)
+        added(j)
 
     def summed(j):
         for c in b2[j]:
@@ -587,8 +620,8 @@
 def on_device(features, block_values, block_coords, live_blocks, weight, bias, cotangent):
     blocks, coords = block_values[0, 0], block_coords[0, 0]
     nodes = features.shape[0] * lax.axis_size("col")
-    x_t = gather_rows(features.T).reshape(256, 2048)
-    part = forward_products(coords, live_blocks, blocks, x_t)
+    x_t, blocks, coords = gather_rows(features.T, blocks, coords)
+    part = forward_products(coords, live_blocks, blocks, x_t.reshape(256, 2048))
     out, grads, term = middle(part, cotangent, weight, bias[None], nodes**-0.5)
     part_x, out, grad_weight, grad_bias = backward_products(
         coords, live_blocks, blocks, grads.reshape(64, 256, 128), out, term

time: 154 us -> 129 us (0.84)
  the two profiles are of different devices: /device:TPU:1 before, /device:TPU:32 now
where the time goes in v3:
time: 129 us
  Pallas kernels  126 us (98%)
  local copies, waits for them, and re-layouts  2.26 us (2%)
  between operations  1.37 us (1%)
    pallas_call x1, Pallas kernels, middle(): pl.pallas_call(functools.partial(middle_kernel, norm), out_shape=(jax.Sha...  68.3 us
    pallas_call x1, Pallas kernels, finish(): pl.pallas_call(finish_kernel, out_shape=jax.ShapeDtypeStruct((32, 2048),...  24.1 us
    pallas_call x1, Pallas kernels, gather_rows(): pl.pallas_call(gather_rows_kernel, out_shape=(jax.ShapeDtypeStruct((8, wi...  22.3 us
    pallas_call x1, Pallas kernels, forward_products(): pl.pallas_call(forward_kernel, out_shape=jax.ShapeDtypeStruct((2, 16, 256...  5.69 us
    pallas_call x1, Pallas kernels, backward_products(): pl.pallas_call(backward_kernel, out_shape=(jax.ShapeDtypeStruct((256, 204...  5.22 us

profile of v3, /device:TPU:32, one launch (start us, length us, event | category | flops | bytes accessed | tf_op | source)
XLA Modules:
  0.0 129.3 jit_solution(11468482737912006311)
XLA Ops:
  1.3 0.0 copy-start
  1.3 0.9 copy-done
  2.2 0.0 copy-start.3
  2.2 0.7 copy-done.3
  2.9 22.3 %gather_features.1 = (bf16[8,32,2048]{2,1,0:T(8,128)(2,1)S(1)}, bf16[256,128,128]{2,1,0:T(8,128)(2,1)S(1)}, s32[2,256]{1,0:T(2,128)S(1)}) custom-call(bf16[32,2048]{1,0:T(8,128)(2,1)S(1)} %bitcast.13, bf16[256,128,128]{2,1,0:T(8,128)(2,1)} %bitcast.16, s32[2,256]{1,0:T(2,128)S(1)} %bitcast.14), custom_call_target="tpu_custom_call" | custom-call | tf_op jit(solution)/shard_map/gather_features/pallas_call | solution.py:141
  25.2 0.0 copy-start.1
  25.2 0.0 copy-start.2
  25.2 0.0 copy-start.4
  25.2 5.7 %forward_products.1.part = bf16[2,16,256,256]{3,2,1,0:T(8,128)(2,1)S(1)} custom-call(s32[2,256]{1,0:T(2,128)S(1)} %get-tuple-element.14.coords, s32[1,1]{1,0:T(1,128)S(6)} %copy.12.live, bf16[256,128,128]{2,1,0:T(8,128)(2,1)S(1)} %get-tuple-element.15.a_ref, bf16[256,2048]{1,0:T(8,128)(2,1)S(1)} %bitcast.10), custom_call_target="tpu_custom_call" | custom-call | tf_op jit(solution)/shard_map/forward_products/pallas_call | solution.py:196
  30.9 0.0 copy-done.1
  31.0 0.0 copy-done.2
  31.0 0.0 copy-done.4
  31.0 68.3 %layer.1 = (bf16[256,256]{1,0:T(8,128)(2,1)S(1)}, bf16[32,2,256,128]{3,2,1,0:T(8,128)(2,1)S(1)}, f32[256,384]{1,0:T(8,128)S(1)}) custom-call(bf16[2,16,256,256]{3,2,1,0:T(8,128)(2,1)S(1)} %forward_products.1.part, bf16[256,256]{1,0:T(8,128)(2,1)S(1)} %copy-done.1, bf16[256,256]{1,0:T(8,128)(2,1)S(1)} %copy-done.2, f32[1,256]{1,0:T(1,128)S(1)} %bitcast.15), custom_call_target="tpu_custom_call" | custom-call | tf_op jit(solution)/shard_map/layer/pallas_call | solution.py:448
  99.3 5.2 %backward_products.1 = (bf16[256,2048]{1,0:T(8,128)(2,1)S(1)}, bf16[256,256]{1,0:T(8,128)(2,1)}, f32[256,256]{1,0:T(8,128)}, f32[1,256]{1,0:T(1,128)}) custom-call(s32[2,256]{1,0:T(2,128)S(1)} %get-tuple-element.14.coords, s32[1,1]{1,0:T(1,128)S(6)} %copy.12.live, bf16[256,128,128]{2,1,0:T(8,128)(2,1)S(1)} %get-tuple-element.15.a_ref, ...), custom_call_target="tpu_custom_call" | custom-call | tf_op jit(solution)/shard_map/backward_products/pallas_call | solution.py:513
  104.5 24.1 %finish.1 = bf16[32,2048]{1,0:T(8,128)(2,1)S(1)} custom-call(bf16[8,32,2048]{2,1,0:T(8,128)(2,1)S(1)} %bitcast.11), custom_call_target="tpu_custom_call" | custom-call | tf_op jit(solution)/shard_map/finish/pallas_call | solution.py:596
  128.6 0.7 copy.13
Async XLA Ops:
  1.3 0.9 copy-start
  2.2 0.7 copy-start.3
  25.2 5.7 %copy-start.1 = (bf16[256,256]{1,0:T(8,128)(2,1)S(1)}, bf16[256,256]{1,0:T(8,128)(2,1)}, u32[]{:S(2)}) copy-start(bf16[256,256]{1,0:T(8,128)(2,1)} %cot_ref.1) | copy-start | bytes 393220
  25.2 5.7 %copy-start.2 = (bf16[256,256]{1,0:T(8,128)(2,1)S(1)}, bf16[256,256]{1,0:T(8,128)(2,1)}, u32[]{:S(2)}) copy-start(bf16[256,256]{1,0:T(8,128)(2,1)} %w_ref.1) | copy-start | bytes 393220
  25.2 5.7 %copy-start.4 = (f32[256]{0:T(256)S(1)}, f32[256]{0:T(256)}, u32[]{:S(2)}) copy-start(f32[256]{0:T(256)} %param.12) | copy-start | bytes 3076

commit v4 on v3

--- a/solution.py
+++ b/solution.py
@@ -10,7 +10,7 @@
 MESH = pl.DeviceIdType.MESH
 F32 = jnp.float32
 BF16 = jnp.bfloat16
-UNROLL = 8
+UNROLL = 16
 VMEM = pl.BlockSpec(memory_space=pltpu.VMEM)
 SMEM = pl.BlockSpec(memory_space=pltpu.SMEM)
 ANY = pl.BlockSpec(memory_space=pltpu.HBM)
@@ -77,7 +77,7 @@
         start(copy_to(x_ref.at[h], full_ref.at[mine, h], sends, recvs, 12 + i, across))
         for i, h in enumerate(halves)
     ]
-    firsts = []
+    forwards = []
     for k in range(2):
         me = mine if k == 0 else other
         base = (zh if k == 0 else 1 - zh) * 4
@@ -96,13 +96,9 @@
         l1 = ring(1, 1, left)
         r1 = ring(1, 2, right)
         l0 = ring(0, 3, left)
-        firsts.append((r0, l1, r1, l0, base))
         if k == 0:
             for c in staged:
                 c.start()
-    forwards = []
-    for k in range(2):
-        r0, l1, r1, l0, base = firsts[k]
         from_left = base + rem4(y + 3)
         from_right = base + rem4(y + 1)
         r0.wait_recv()
@@ -237,7 +233,11 @@
     zk = [rem4(zl + k) for k in range(4)]
     order = (2, 1, 3, 0)
     a = {}
-    for k in (2, 1, 3, 0):
+    far = {}
+    for k in order:
+        i = xk[2] * 4 + zk[k]
+        far[k] = start(part.at[1 - core, i], r_a.at[i], twin)
+    for k in (1, 3, 0):
         sl = pl.ds(xk[k] * 4, 4)
         a[k] = start(part.at[1 - core, sl], r_a.at[sl], twin)
 
@@ -255,6 +255,8 @@
 
     def first(k):
         i = xk[2] * 4 + zk[k]
+        far[k].wait_recv()
+        s_a[i] = (part[core, i].astype(F32) + r_a[i].astype(F32)).astype(BF16)
         b1[k] = (
             start(s_a.at[i, top], r_b1l.at[k], right),
             start(s_a.at[i, low], r_b1r.at[k], left),
@@ -286,7 +288,6 @@
         s_b[k] = summed(k).astype(BF16)
         c_z[k] = start(s_b.at[k], r_c.at[k], along[k])
 
-    add_cores(2)
     first(order[0])
     first(order[1])
     add_cores(1)
@@ -548,44 +549,64 @@
     top, low = pl.ds(0, 16), pl.ds(16, 16)
 
     zs = (1 - zh, zh)
-    b1, b2 = [], []
-
-    def first(j):
+    every = pl.ds(0, 16)
+    pieces = ((0, pl.ds(0, 1024)), (0, pl.ds(1024, 1024)), (1, pl.ds(0, 2048)))
+    b1, b2 = {}, {}
+
+    def first(p):
+        j, at = pieces[p]
         i = zs[j] * 4 + yk[2]
-        b1.append(
-            (start(part.at[i, top], r_b1l.at[j], right), start(part.at[i, low], r_b1r.at[j], left))
+        b1[p] = (
+            start(part.at[i, top, at], r_b1l.at[j, every, at], right),
+            start(part.at[i, low, at], r_b1r.at[j, every, at], left),
         )
 
-    def plain(j):
-        b2.append(
-            [
-                start(part.at[zs[j] * 4 + yk[1], low], r_b2l.at[j, low], right),
-                start(part.at[zs[j] * 4 + yk[3], top], r_b2r.at[j, top], left),
-            ]
+    def plain(p):
+        j, at = pieces[p]
+        b2[p] = [
+            start(part.at[zs[j] * 4 + yk[1], low, at], r_b2l.at[j, low, at], right),
+            start(part.at[zs[j] * 4 + yk[3], top, at], r_b2r.at[j, top, at], left),
+        ]
+
+    def added(p):
+        j, at = pieces[p]
+        b1[p][0].wait_recv()
+        s_b1r[j, :, at] = (
+            part[zs[j] * 4 + yk[1], top, at].astype(F32) + r_b1l[j, :, at].astype(F32)
+        ).astype(BF16)
+        b2[p].append(start(s_b1r.at[j, every, at], r_b2l.at[j, top, at], right))
+        b1[p][1].wait_recv()
+        s_b1l[j, :, at] = (
+            part[zs[j] * 4 + yk[3], low, at].astype(F32) + r_b1r[j, :, at].astype(F32)
+        ).astype(BF16)
+        b2[p].append(start(s_b1l.at[j, every, at], r_b2r.at[j, low, at], left))
+
+    def summed(p):
+        j, at = pieces[p]
+        for c in b2[p]:
+            c.wait_recv()
+        return part[zs[j] * 4 + y, :, at].astype(F32) + (
+            r_b2l[j, :, at].astype(F32) + r_b2r[j, :, at].astype(F32)
         )
 
-    def added(j):
-        b1[j][0].wait_recv()
-        s_b1r[j] = (part[zs[j] * 4 + yk[1], top].astype(F32) + r_b1l[j].astype(F32)).astype(BF16)
-        b2[j].append(start(s_b1r.at[j], r_b2l.at[j, top], right))
-        b1[j][1].wait_recv()
-        s_b1l[j] = (part[zs[j] * 4 + yk[3], low].astype(F32) + r_b1r[j].astype(F32)).astype(BF16)
-        b2[j].append(start(s_b1l.at[j], r_b2r.at[j, low], left))
-
-    for j in range(2):
-        first(j)
-        plain(j)
-        added(j)
-
-    def summed(j):
-        for c in b2[j]:
-            c.wait_recv()
-        return part[zs[j] * 4 + y].astype(F32) + (r_b2l[j].astype(F32) + r_b2r[j].astype(F32))
-
-    s_b[...] = summed(0).astype(BF16)
-    cz = start(s_b, r_c, across)
-    own = summed(1)
-    cz.wait_recv()
+    def over(p):
+        at = pieces[p][1]
+        s_b[:, at] = summed(p).astype(BF16)
+        return start(s_b.at[pl.ds(0, 32), at], r_c.at[pl.ds(0, 32), at], across)
+
+    first(0)
+    plain(0)
+    first(1)
+    added(0)
+    plain(1)
+    added(1)
+    first(2)
+    plain(2)
+    cz = [over(0), over(1)]
+    added(2)
+    own = summed(2)
+    for c in cz:
+        c.wait_recv()
     gx_ref[...] = (own + r_c[...].astype(F32)).astype(BF16)
     for c in started:
         c.wait_send()
@@ -607,8 +628,8 @@
             pltpu.VMEM(whole, BF16),
             pltpu.VMEM(whole[1:], BF16),
             pltpu.VMEM(whole[1:], BF16),
-            pltpu.SemaphoreType.DMA((16,)),
-            pltpu.SemaphoreType.DMA((16,)),
+            pltpu.SemaphoreType.DMA((24,)),
+            pltpu.SemaphoreType.DMA((24,)),
         ],
         compiler_params=pltpu.CompilerParams(
             collective_id=2, has_side_effects=True, vmem_limit_bytes=FINISH_VMEM

time: 129 us -> 124 us (0.961)
  the two profiles are of different devices: /device:TPU:32 before, /device:TPU:1 now
where the time goes in v4:
time: 124 us; the launch traced here: 122 us
  Pallas kernels  118 us (95%)
  local copies, waits for them, and re-layouts  2.26 us (2%)
  between operations  1.37 us (1%)
    pallas_call x1, Pallas kernels, middle(): pl.pallas_call(functools.partial(middle_kernel, norm), out_shape=(jax.Sha...  74.1 us
    pallas_call x1, Pallas kernels, gather_rows(): pl.pallas_call(gather_rows_kernel, out_shape=(jax.ShapeDtypeStruct((8, wi...  19 us
    pallas_call x1, Pallas kernels, finish(): pl.pallas_call(finish_kernel, out_shape=jax.ShapeDtypeStruct((32, 2048),...  18.9 us
    pallas_call x1, Pallas kernels, forward_products(): pl.pallas_call(forward_kernel, out_shape=jax.ShapeDtypeStruct((2, 16, 256...  3.38 us
    pallas_call x1, Pallas kernels, backward_products(): pl.pallas_call(backward_kernel, out_shape=(jax.ShapeDtypeStruct((256, 204...  2.91 us

profile of v4, /device:TPU:1, one launch (start us, length us, event | category | flops | bytes accessed | tf_op | source)
XLA Modules:
  0.0 122.0 jit_solution(15647668390916698003)
XLA Ops:
  1.3 0.0 copy-start
  1.3 0.9 copy-done
  2.2 0.0 copy-start.3
  2.2 0.7 copy-done.3
  2.9 19.0 %gather_features.1 = (bf16[8,32,2048]{2,1,0:T(8,128)(2,1)S(1)}, bf16[256,128,128]{2,1,0:T(8,128)(2,1)S(1)}, s32[2,256]{1,0:T(2,128)S(1)}) custom-call(bf16[32,2048]{1,0:T(8,128)(2,1)S(1)} %bitcast.13, bf16[256,128,128]{2,1,0:T(8,128)(2,1)} %bitcast.16, s32[2,256]{1,0:T(2,128)S(1)} %bitcast.14), custom_call_target="tpu_custom_call" | custom-call | tf_op jit(solution)/shard_map/gather_features/pallas_call | solution.py:137
  21.9 0.0 copy-start.1
  21.9 0.0 copy-start.2
  21.9 0.0 copy-start.4
  21.9 3.4 %forward_products.1.part = bf16[2,16,256,256]{3,2,1,0:T(8,128)(2,1)S(1)} custom-call(s32[2,256]{1,0:T(2,128)S(1)} %get-tuple-element.14.coords, s32[1,1]{1,0:T(1,128)S(6)} %copy.12.live, bf16[256,128,128]{2,1,0:T(8,128)(2,1)S(1)} %get-tuple-element.15.a_ref, bf16[256,2048]{1,0:T(8,128)(2,1)S(1)} %bitcast.10), custom_call_target="tpu_custom_call" | custom-call | tf_op jit(solution)/shard_map/forward_products/pallas_call | solution.py:192
  25.3 0.0 copy-done.1
  25.3 0.0 copy-done.2
  25.3 0.0 copy-done.4
  25.4 74.1 %layer.1 = (bf16[256,256]{1,0:T(8,128)(2,1)S(1)}, bf16[32,2,256,128]{3,2,1,0:T(8,128)(2,1)S(1)}, f32[256,384]{1,0:T(8,128)S(1)}) custom-call(bf16[2,16,256,256]{3,2,1,0:T(8,128)(2,1)S(1)} %forward_products.1.part, bf16[256,256]{1,0:T(8,128)(2,1)S(1)} %copy-done.1, bf16[256,256]{1,0:T(8,128)(2,1)S(1)} %copy-done.2, f32[1,256]{1,0:T(1,128)S(1)} %bitcast.15), custom_call_target="tpu_custom_call" | custom-call | tf_op jit(solution)/shard_map/layer/pallas_call | solution.py:449
  99.5 2.9 %backward_products.1 = (bf16[256,2048]{1,0:T(8,128)(2,1)S(1)}, bf16[256,256]{1,0:T(8,128)(2,1)}, f32[256,256]{1,0:T(8,128)}, f32[1,256]{1,0:T(1,128)}) custom-call(s32[2,256]{1,0:T(2,128)S(1)} %get-tuple-element.14.coords, s32[1,1]{1,0:T(1,128)S(6)} %copy.12.live, bf16[256,128,128]{2,1,0:T(8,128)(2,1)S(1)} %get-tuple-element.15.a_ref, ...), custom_call_target="tpu_custom_call" | custom-call | tf_op jit(solution)/shard_map/backward_products/pallas_call | solution.py:514
  102.4 18.9 %finish.1 = bf16[32,2048]{1,0:T(8,128)(2,1)S(1)} custom-call(bf16[8,32,2048]{2,1,0:T(8,128)(2,1)S(1)} %bitcast.11), custom_call_target="tpu_custom_call" | custom-call | tf_op jit(solution)/shard_map/finish/pallas_call | solution.py:617
  121.3 0.7 copy.13
Async XLA Ops:
  1.3 0.9 copy-start
  2.2 0.7 copy-start.3
  21.9 3.4 %copy-start.1 = (bf16[256,256]{1,0:T(8,128)(2,1)S(1)}, bf16[256,256]{1,0:T(8,128)(2,1)}, u32[]{:S(2)}) copy-start(bf16[256,256]{1,0:T(8,128)(2,1)} %cot_ref.1) | copy-start | bytes 393220
  21.9 3.4 %copy-start.2 = (bf16[256,256]{1,0:T(8,128)(2,1)S(1)}, bf16[256,256]{1,0:T(8,128)(2,1)}, u32[]{:S(2)}) copy-start(bf16[256,256]{1,0:T(8,128)(2,1)} %w_ref.1) | copy-start | bytes 393220
  21.9 3.4 %copy-start.4 = (f32[256]{0:T(256)S(1)}, f32[256]{0:T(256)}, u32[]{:S(2)}) copy-start(f32[256]{0:T(256)} %param.12) | copy-start | bytes 3076

commit v5 on v4

--- a/solution.py
+++ b/solution.py
@@ -10,7 +10,7 @@
 MESH = pl.DeviceIdType.MESH
 F32 = jnp.float32
 BF16 = jnp.bfloat16
-UNROLL = 16
+UNROLL = 32
 VMEM = pl.BlockSpec(memory_space=pltpu.VMEM)
 SMEM = pl.BlockSpec(memory_space=pltpu.SMEM)
 ANY = pl.BlockSpec(memory_space=pltpu.HBM)

time: 124 us -> 122 us (0.984); the launches traced: 122 us -> 122 us
    pallas_call x1, Pallas kernels: 74.1 us -> 67.4 us  [middle(): pl.pallas_call(functools.partial(middle_kernel, norm), out_shape=(jax.Sha...]
    pallas_call x1, Pallas kernels: 2.91 us -> 7.62 us  [backward_products(): pl.pallas_call(backward_kernel, out_shape=(jax.ShapeDtypeStruct((256, 204...]
    pallas_call x1, Pallas kernels: 3.38 us -> 8.01 us  [forward_products(): pl.pallas_call(forward_kernel, out_shape=jax.ShapeDtypeStruct((2, 16, 256...]
    pallas_call x1, Pallas kernels: 18.9 us -> 16.2 us  [finish(): pl.pallas_call(finish_kernel, out_shape=jax.ShapeDtypeStruct((32, 2048),...]
where the time goes in v5:
time: 122 us
  Pallas kernels  118 us (97%)
  local copies, waits for them, and re-layouts  2.26 us (2%)
  between operations  1.37 us (1%)
    pallas_call x1, Pallas kernels, middle(): pl.pallas_call(functools.partial(middle_kernel, norm), out_shape=(jax.Sha...  67.4 us
    pallas_call x1, Pallas kernels, gather_rows(): pl.pallas_call(gather_rows_kernel, out_shape=(jax.ShapeDtypeStruct((8, wi...  19 us
    pallas_call x1, Pallas kernels, finish(): pl.pallas_call(finish_kernel, out_shape=jax.ShapeDtypeStruct((32, 2048),...  16.2 us
    pallas_call x1, Pallas kernels, forward_products(): pl.pallas_call(forward_kernel, out_shape=jax.ShapeDtypeStruct((2, 16, 256...  8.01 us
    pallas_call x1, Pallas kernels, backward_products(): pl.pallas_call(backward_kernel, out_shape=(jax.ShapeDtypeStruct((256, 204...  7.62 us

profile of v5, /device:TPU:1, one launch (start us, length us, event | category | flops | bytes accessed | tf_op | source)
XLA Modules:
  0.0 121.9 jit_solution(1819592091314870053)
XLA Ops:
  1.3 0.0 copy-start
  1.3 0.9 copy-done
  2.2 0.0 copy-start.3
  2.2 0.7 copy-done.3
  2.9 19.0 %gather_features.1 = (bf16[8,32,2048]{2,1,0:T(8,128)(2,1)S(1)}, bf16[256,128,128]{2,1,0:T(8,128)(2,1)S(1)}, s32[2,256]{1,0:T(2,128)S(1)}) custom-call(bf16[32,2048]{1,0:T(8,128)(2,1)S(1)} %bitcast.13, bf16[256,128,128]{2,1,0:T(8,128)(2,1)} %bitcast.16, s32[2,256]{1,0:T(2,128)S(1)} %bitcast.14), custom_call_target="tpu_custom_call" | custom-call | tf_op jit(solution)/shard_map/gather_features/pallas_call | solution.py:137
  21.9 0.0 copy-start.1
  21.9 0.0 copy-start.2
  21.9 0.0 copy-start.4
  21.9 8.0 %forward_products.1.part = bf16[2,16,256,256]{3,2,1,0:T(8,128)(2,1)S(1)} custom-call(s32[2,256]{1,0:T(2,128)S(1)} %get-tuple-element.14.coords, s32[1,1]{1,0:T(1,128)S(6)} %copy.12.live, bf16[256,128,128]{2,1,0:T(8,128)(2,1)S(1)} %get-tuple-element.15.a_ref, bf16[256,2048]{1,0:T(8,128)(2,1)S(1)} %bitcast.10), custom_call_target="tpu_custom_call" | custom-call | tf_op jit(solution)/shard_map/forward_products/pallas_call | solution.py:192
  30.0 0.0 copy-done.1
  30.0 0.0 copy-done.2
  30.0 0.0 copy-done.4
  30.0 67.4 %layer.1 = (bf16[256,256]{1,0:T(8,128)(2,1)S(1)}, bf16[32,2,256,128]{3,2,1,0:T(8,128)(2,1)S(1)}, f32[256,384]{1,0:T(8,128)S(1)}) custom-call(bf16[2,16,256,256]{3,2,1,0:T(8,128)(2,1)S(1)} %forward_products.1.part, bf16[256,256]{1,0:T(8,128)(2,1)S(1)} %copy-done.1, bf16[256,256]{1,0:T(8,128)(2,1)S(1)} %copy-done.2, f32[1,256]{1,0:T(1,128)S(1)} %bitcast.15), custom_call_target="tpu_custom_call" | custom-call | tf_op jit(solution)/shard_map/layer/pallas_call | solution.py:449
  97.4 7.6 %backward_products.1 = (bf16[256,2048]{1,0:T(8,128)(2,1)S(1)}, bf16[256,256]{1,0:T(8,128)(2,1)}, f32[256,256]{1,0:T(8,128)}, f32[1,256]{1,0:T(1,128)}) custom-call(s32[2,256]{1,0:T(2,128)S(1)} %get-tuple-element.14.coords, s32[1,1]{1,0:T(1,128)S(6)} %copy.12.live, bf16[256,128,128]{2,1,0:T(8,128)(2,1)S(1)} %get-tuple-element.15.a_ref, ...), custom_call_target="tpu_custom_call" | custom-call | tf_op jit(solution)/shard_map/backward_products/pallas_call | solution.py:514
  105.0 16.2 %finish.1 = bf16[32,2048]{1,0:T(8,128)(2,1)S(1)} custom-call(bf16[8,32,2048]{2,1,0:T(8,128)(2,1)S(1)} %bitcast.11), custom_call_target="tpu_custom_call" | custom-call | tf_op jit(solution)/shard_map/finish/pallas_call | solution.py:617
  121.2 0.7 copy.13
Async XLA Ops:
  1.3 0.9 copy-start
  2.2 0.7 copy-start.3
  21.9 8.1 %copy-start.1 = (bf16[256,256]{1,0:T(8,128)(2,1)S(1)}, bf16[256,256]{1,0:T(8,128)(2,1)}, u32[]{:S(2)}) copy-start(bf16[256,256]{1,0:T(8,128)(2,1)} %cot_ref.1) | copy-start | bytes 393220
  21.9 8.1 %copy-start.2 = (bf16[256,256]{1,0:T(8,128)(2,1)S(1)}, bf16[256,256]{1,0:T(8,128)(2,1)}, u32[]{:S(2)}) copy-start(bf16[256,256]{1,0:T(8,128)(2,1)} %w_ref.1) | copy-start | bytes 393220
  21.9 8.0 %copy-start.4 = (f32[256]{0:T(256)S(1)}, f32[256]{0:T(256)}, u32[]{:S(2)}) copy-start(f32[256]{0:T(256)} %param.12) | copy-start | bytes 3076
